TPU v7x, 256 devices: a whole 4x4x8 slice. The times are simulated.
256 devices in a mesh: gx: 8 (over y, z_hi), gy: 8 (over x, core), gz: 4 (over z_lo).
Axes of the slice: x: 4, y: 4, z: 8 (z_hi: 2, z_lo: 4; z = z_hi * 4 + z_lo), core: 2. Of those that a mesh axis runs over, the one named last changes fastest.
Arguments:
- volume: bfloat16 [32, 64, 64, 128], P('gz', 'gx', 'gy'), may hold values from -6 to 6
- cotangent: bfloat16 [32, 64, 64, 128], P('gz', 'gx', 'gy'), may hold values from -0.0390625 to 0.0390625
- w_conv: bfloat16 [128, 27, 128], replicated, may hold values from -0.109375 to 0.109375
- w_down: bfloat16 [8, 128, 512], replicated, may hold values from -0.25 to 0.25
- w_bottle: bfloat16 [512, 27, 512], P(None, None, 'gz'), may hold values from -0.0546875 to 0.0546875
- w_up: bfloat16 [8, 512, 128], replicated, may hold values from -0.375 to 0.375
Outputs:
- output: bfloat16 [32, 64, 64, 128], P('gz', 'gx', 'gy')
- grad_conv: float32 [128, 27, 128], P(('gx', 'gy'))
- grad_bottle: float32 [512, 27, 512], P(('gx', 'gy'), None, 'gz')
All inputs are finite; a program needn't handle non-finite values.
Results may differ from a plain program's by a relative error of at most 0.015.
Values may be sent and summed in bfloat16 or wider, within the bound.
A program may use at most 64 MiB of HBM per device.

v0:
```python
import jax
import jax.numpy as jnp
from jax import lax
from jax.sharding import PartitionSpec as P


def with_halo(cells, sides, width):
    for axis, dim in sides:
        count = lax.axis_size(axis)
        ends = count - 1
        head = lax.slice_in_dim(cells, 0, width, axis=dim)
        tail = lax.slice_in_dim(cells, cells.shape[dim] - width, cells.shape[dim], axis=dim)
        cells = jnp.concatenate(
            [
                lax.ppermute(tail, axis, [(i, (i + 1) % count) for i in range(ends)]),
                cells,
                lax.ppermute(head, axis, [((i + 1) % count, i) for i in range(ends)]),
            ],
            axis=dim,
        )
    return cells


def silu_slope(values):
    sig = jax.nn.sigmoid(values)
    return sig * (1.0 + values * (1.0 - sig))


def conv_forward(padded, weight, extent):
    size_z, size_x, size_y = extent
    count_cells = size_z * size_x * size_y
    summed = jnp.zeros((count_cells, weight.shape[2]), jnp.float32)
    for tap_index in range(27):
        shift_z, shift_x, shift_y = (tap_index // 9, tap_index // 3 % 3, tap_index % 3)
        window = padded[
            shift_z : shift_z + size_z, shift_x : shift_x + size_x, shift_y : shift_y + size_y, :
        ]
        window = window.reshape(count_cells, padded.shape[3])
        summed = summed + jnp.dot(
            window, weight[:, tap_index, :], preferred_element_type=jnp.float32
        )
    return summed.reshape(size_z, size_x, size_y, weight.shape[2])


def conv_weight_grad(padded, gradient, extent):
    size_z, size_x, size_y = extent
    count_cells = size_z * size_x * size_y
    flat_gradient = gradient.reshape(count_cells, gradient.shape[3])
    pieces = []
    for tap_index in range(27):
        shift_z, shift_x, shift_y = (tap_index // 9, tap_index // 3 % 3, tap_index % 3)
        window = padded[
            shift_z : shift_z + size_z, shift_x : shift_x + size_x, shift_y : shift_y + size_y, :
        ]
        window = window.reshape(count_cells, padded.shape[3])
        pieces.append(
            lax.dot_general(
                window, flat_gradient, (((0,), (0,)), ((), ())), preferred_element_type=jnp.float32
            )
        )
    return jnp.stack(pieces, axis=1)


def conv_input_grad(padded, weight, extent):
    size_z, size_x, size_y = extent
    count_cells = size_z * size_x * size_y
    summed = jnp.zeros((count_cells, weight.shape[0]), jnp.float32)
    for tap_index in range(27):
        shift_z, shift_x, shift_y = (2 - tap_index // 9, 2 - tap_index // 3 % 3, 2 - tap_index % 3)
        window = padded[
            shift_z : shift_z + size_z, shift_x : shift_x + size_x, shift_y : shift_y + size_y, :
        ]
        window = window.reshape(count_cells, padded.shape[3])
        summed = summed + lax.dot_general(
            window,
            weight[:, tap_index, :],
            (((1,), (1,)), ((), ())),
            preferred_element_type=jnp.float32,
        )
    return summed.reshape(size_z, size_x, size_y, weight.shape[0])


def pool_features(fine, kernel):
    size_z, size_x, size_y, channels = fine.shape
    blocks = fine.reshape(size_z // 2, 2, size_x // 2, 2, size_y // 2, 2, channels)
    kernel_cube = kernel.reshape(2, 2, 2, kernel.shape[1], kernel.shape[2])
    return jnp.einsum(
        "zaxbycf,abcfg->zxyg", blocks, kernel_cube, preferred_element_type=jnp.float32
    )


def pool_adjoint(coarse_in, kernel):
    size_z, size_x, size_y, wide_channels = coarse_in.shape
    kernel_cube = kernel.reshape(2, 2, 2, kernel.shape[1], kernel.shape[2])
    result = jnp.einsum(
        "zxyg,abcfg->zaxbycf", coarse_in, kernel_cube, preferred_element_type=jnp.float32
    )
    return result.reshape(2 * size_z, 2 * size_x, 2 * size_y, kernel.shape[1])


def lift_features(coarse_in, kernel):
    size_z, size_x, size_y, wide_channels = coarse_in.shape
    kernel_cube = kernel.reshape(2, 2, 2, kernel.shape[1], kernel.shape[2])
    result = jnp.einsum(
        "zxyg,abcgf->zaxbycf", coarse_in, kernel_cube, preferred_element_type=jnp.float32
    )
    return result.reshape(2 * size_z, 2 * size_x, 2 * size_y, kernel.shape[2])


def lift_adjoint(fine, kernel):
    size_z, size_x, size_y, channels = fine.shape
    blocks = fine.reshape(size_z // 2, 2, size_x // 2, 2, size_y // 2, 2, channels)
    kernel_cube = kernel.reshape(2, 2, 2, kernel.shape[1], kernel.shape[2])
    return jnp.einsum(
        "zaxbycf,abcgf->zxyg", blocks, kernel_cube, preferred_element_type=jnp.float32
    )


def body(volume, cotangent, w_conv, w_down, w_bottle, w_up):
    size_z, size_x, size_y, channels = volume.shape
    group_channels = w_bottle.shape[2]
    half_x = size_x // 2
    half_y = size_y // 2
    padded = with_halo(volume, (("gx", 1), ("gy", 2), ("gz", 0)), 1)
    pre_hidden = conv_forward(padded, w_conv, (size_z, size_x, size_y))
    hidden = jax.nn.silu(pre_hidden).astype(jnp.bfloat16)
    hidden_slope = silu_slope(pre_hidden)
    coarse = pool_features(hidden, w_down).astype(jnp.bfloat16)
    stacked = lax.all_gather(coarse, "gz", axis=0, tiled=True)
    rimmed = with_halo(stacked, (("gx", 1), ("gy", 2)), 1)
    column_z = rimmed.shape[0]
    coarse_pad = jnp.pad(rimmed, ((1, 1), (0, 0), (0, 0), (0, 0)))
    pre_bottle = conv_forward(coarse_pad, w_bottle, (column_z, half_x, half_y))
    bottle = jax.nn.silu(pre_bottle).astype(jnp.bfloat16)
    bottle_slope = silu_slope(pre_bottle)
    own_start = lax.axis_index("gz") * group_channels
    own_up = lax.dynamic_slice_in_dim(w_up, own_start, group_channels, 1)
    lifted = lax.psum_scatter(
        lift_features(bottle, own_up).astype(jnp.bfloat16), "gz", scatter_dimension=0, tiled=True
    ).astype(jnp.float32)
    output = (lifted + hidden.astype(jnp.float32)).astype(jnp.bfloat16)
    back_bottle = lift_adjoint(cotangent, w_up).astype(jnp.bfloat16)
    split_grad = lax.all_to_all(back_bottle, "gz", split_axis=3, concat_axis=0, tiled=True)
    bottle_grad = (split_grad.astype(jnp.float32) * bottle_slope).astype(jnp.bfloat16)
    grad_bottle = lax.psum_scatter(
        conv_weight_grad(coarse_pad, bottle_grad, (column_z, half_x, half_y)),
        ("gx", "gy"),
        scatter_dimension=0,
        tiled=True,
    )
    grad_rimmed = with_halo(bottle_grad, (("gx", 1), ("gy", 2)), 1)
    grad_pad = jnp.pad(grad_rimmed, ((1, 1), (0, 0), (0, 0), (0, 0)))
    coarse_grad = lax.psum_scatter(
        conv_input_grad(
            grad_pad, w_bottle, (lax.axis_size("gz") * (size_z // 2), half_x, half_y)
        ).astype(jnp.bfloat16),
        "gz",
        scatter_dimension=0,
        tiled=True,
    )
    hidden_grad = (
        (pool_adjoint(coarse_grad, w_down) + cotangent.astype(jnp.float32)) * hidden_slope
    ).astype(jnp.bfloat16)
    full_term = conv_weight_grad(padded, hidden_grad, (size_z, size_x, size_y))
    depth_summed = lax.psum(full_term.astype(jnp.bfloat16), "gz").astype(jnp.float32)
    grad_conv = lax.psum_scatter(depth_summed, ("gx", "gy"), scatter_dimension=0, tiled=True)
    return (output, grad_conv, grad_bottle)


def solution(mesh):
    in_specs = (
        P("gz", "gx", "gy", None),
        P("gz", "gx", "gy", None),
        P(),
        P(),
        P(None, None, "gz"),
        P(),
    )
    out_specs = (
        P("gz", "gx", "gy", None),
        P(("gx", "gy"), None, None),
        P(("gx", "gy"), None, "gz"),
    )
    return jax.shard_map(body, mesh=mesh, in_specs=in_specs, out_specs=out_specs, check_vma=False)
```

profile of v0, /device:TPU:0, one launch (start us, length us, event | category | flops | bytes accessed | tf_op | source)
XLA Modules:
  0.0 818.0 jit_solution(18367334462036747407)
XLA Ops:
  10.1 8.5 %collective-permute-start = (bf16[8,1,8,128]{3,2,1,0:T(8,128)(2,1)S(1)}, bf16[8,1,8,128]{3,2,1,0:T(8,128)(2,1)S(1)}, u32[]{:S(2)}, u32[]{:S(2)}) collective-permute-start(bf16[8,1,8,128]{3,2,1,0:T(8,128)(2,1)S(1)} %get-tuple-element.94), channel_id=1, source_target_pairs={{0,32},{32,64},{64,96},{96,128},{128,160},{160,192},{192,224},{1,3... | collective-permute-start | bytes 49160 | tf_op jit(solution)/shard_map/ppermute | solution.py:15
  20.0 1.9 copy.315
  21.9 4.8 reshape.498
  26.7 4.2 all-to-all-start
  35.9 2.6 collective-permute-done.3
  38.5 3.9 collective-permute-start.4
  45.4 3.1 collective-permute-done.5
  55.1 14.3 %all_gather.3 = bf16[16,4,4,512]{3,2,1,0:T(4,128)(2,1)S(1)} all-gather(bf16[4,4,4,512]{3,2,1,0:T(4,128)(2,1)S(1)} %fusion.33), channel_id=1, replica_groups=mesh['gx'=8,'gy'=8,'gz'=4] {'gz'}, dimensions={0}, use_global_device_ids=true | all-gather | bytes 327680 | tf_op jit(solution)/shard_map/all_gather | solution.py:129
  70.1 8.6 %collective-permute-start.6 = (bf16[16,1,4,512]{3,0,2,1:T(8,128)(2,1)}, bf16[16,1,4,512]{3,0,2,1:T(8,128)(2,1)}, u32[]{:S(2)}, u32[]{:S(2)}) collective-permute-start(bf16[16,1,4,512]{3,0,2,1:T(8,128)(2,1)} %copy.428), channel_id=1, source_target_pairs={{0,32},{32,64},{64,96},{96,128},{128,160},{160,192},{192,224},{1,3... | collective-permute-start | bytes 196616 | tf_op jit(solution)/shard_map/ppermute | solution.py:15
  82.1 5.3 reshape.499
  92.8 1.9 collective-permute-start.8
  96.0 2.7 convert_bitcast_fusion
  98.6 2.6 copy.316
  101.2 4.2 copy.332
  116.8 2.0 fusion.356
  121.5 1.9 copy.310
  125.1 1.9 copy.309
  128.7 1.9 copy.308
  132.3 1.9 copy.307
  135.9 1.9 copy.306
  139.5 1.9 copy.305
  143.1 1.9 copy.304
  146.6 1.9 copy.303
  150.2 1.9 copy.292
  157.4 1.9 copy.290
  187.7 6.8 collective-permute-start.10
  204.1 3.8 collective-permute-start.12
  209.3 4.1 collective-permute-done.13
  229.4 44.6 %all-reduce.10.cloned.1.call-done = bf16[16,4,4,512]{3,2,1,0:T(4,128)(2,1)} async-done(((bf16[16,4,4,512]{3,2,1,0:T(4,128)(2,1)}), bf16[16,4,4,512]{3,2,1,0:T(4,128)(2,1)}) %all-reduce.10.cloned.1.call-update) | async-done | bytes 262160
  275.4 26.7 %reduce-scatter.4.cloned.1.call-done = bf16[8,8,8,128]{3,2,1,0:T(8,128)(2,1)} async-done(((bf16[32,8,8,128]{3,2,1,0:T(8,128)(2,1)}), bf16[8,8,8,128]{3,2,1,0:T(8,128)(2,1)}) %reduce-scatter.4.cloned.1.call-update) | async-done | bytes 131088 | tf_op jit(solution)/shard_map/reduce_scatter | solution.py:138
  317.8 55.8 %all-reduce.8.cloned.1.call-done = bf16[128,27,128]{2,0,1:T(8,128)(2,1)} async-done(((bf16[128,27,128]{2,0,1:T(8,128)(2,1)}), bf16[128,27,128]{2,0,1:T(8,128)(2,1)}) %all-reduce.8.cloned.1.call-update) | async-done | bytes 884752 | tf_op jit(solution)/shard_map/psum | solution.py:165
  373.6 436.3 %all-reduce.11 = f32[128,27,128]{2,0,1:T(8,128)S(1)} all-reduce(bf16[128,27,128]{2,0,1:T(8,128)(2,1)} %all-reduce.8.cloned.1.call-done), channel_id=4, replica_groups=mesh['gx'=8,'gy'=8,'gz'=4] {'gx','gy'}, use_global_device_ids=true, to_apply=%region_3.4.clone | all-reduce | flops 442368 | bytes 2654208
  (410 shorter events, 131.6 us)
Async XLA Ops:
  8.8 23.4 %collective-permute-start.1 = (bf16[8,1,8,128]{3,2,1,0:T(8,128)(2,1)S(1)}, bf16[8,1,8,128]{3,2,1,0:T(8,128)(2,1)S(1)}, u32[]{:S(2)}, u32[]{:S(2)}) collective-permute-start(bf16[8,1,8,128]{3,2,1,0:T(8,128)(2,1)S(1)} %get-tuple-element.93), channel_id=1, source_target_pairs={{32,0},{64,32},{96,64},{128,96},{160,128},{192,160},{224,192},{33,... | collective-permute-start | bytes 49160 | tf_op jit(solution)/shard_map/ppermute | solution.py:17
  10.1 22.0 %collective-permute-start = (bf16[8,1,8,128]{3,2,1,0:T(8,128)(2,1)S(1)}, bf16[8,1,8,128]{3,2,1,0:T(8,128)(2,1)S(1)}, u32[]{:S(2)}, u32[]{:S(2)}) collective-permute-start(bf16[8,1,8,128]{3,2,1,0:T(8,128)(2,1)S(1)} %get-tuple-element.94), channel_id=1, source_target_pairs={{0,32},{32,64},{64,96},{96,128},{128,160},{160,192},{192,224},{1,3... | collective-permute-start | bytes 49160 | tf_op jit(solution)/shard_map/ppermute | solution.py:15
  20.0 12.1 %copy-start.10 = (bf16[8,8,8,128]{3,2,1,0:T(8,128)(2,1)S(1)}, bf16[8,8,8,128]{3,2,1,0:T(8,128)(2,1)}, u32[]{:S(2)}) copy-start(bf16[8,8,8,128]{3,2,1,0:T(8,128)(2,1)} %param.6) | copy-start | bytes 393220
  26.7 55.4 %all-to-all-start = ((bf16[4,2,4096]{2,1,0:T(2,128)(2,1)}), bf16[4,2,4096]{2,1,0:T(2,128)(2,1)}, u32[]{:S(2)}, u32[]{:S(2)}) async-start(bf16[4,2,4096]{2,1,0:T(2,128)(2,1)} %reshape.498), calls=%async_computation.1 | async-start | bytes 131072 | tf_op jit(solution)/shard_map/all_to_all | solution.py:143
  30.9 243.1 %all-reduce.10.cloned.1.call-start = ((), (), s32[]{:S(2)}) async-start(), calls=%async_computation.6 | async-start | bytes 524288
  32.2 12.1 %copy-start.60 = (bf16[8,9,8,128]{3,2,1,0:T(8,128)(2,1)}, bf16[8,9,8,128]{3,2,1,0:T(8,128)(2,1)S(1)}, u32[]{:S(2)}) copy-start(bf16[8,9,8,128]{3,2,1,0:T(8,128)(2,1)S(1)} %get-tuple-element.90) | copy-start | bytes 442372
  32.3 13.1 %copy-start.51 = (bf16[8,9,8,128]{3,2,1,0:T(8,128)(2,1)}, bf16[8,9,8,128]{3,2,1,0:T(8,128)(2,1)S(1)}, u32[]{:S(2)}) copy-start(bf16[8,9,8,128]{3,2,1,0:T(8,128)(2,1)S(1)} %get-tuple-element.115) | copy-start | bytes 442372
  32.4 3.6 collective-permute-start.2
  33.7 4.8 collective-permute-start.3
  38.5 6.8 collective-permute-start.4
  42.5 6.0 collective-permute-start.5
  69.4 12.7 %copy-start.6 = (bf16[16,4,4,512]{3,2,1,0:T(4,128)(2,1)}, bf16[16,4,4,512]{3,2,1,0:T(4,128)(2,1)S(1)}, u32[]{:S(2)}) copy-start(bf16[16,4,4,512]{3,2,1,0:T(4,128)(2,1)S(1)} %all_gather.3) | copy-start | bytes 786436
  70.1 17.3 %collective-permute-start.6 = (bf16[16,1,4,512]{3,0,2,1:T(8,128)(2,1)}, bf16[16,1,4,512]{3,0,2,1:T(8,128)(2,1)}, u32[]{:S(2)}, u32[]{:S(2)}) collective-permute-start(bf16[16,1,4,512]{3,0,2,1:T(8,128)(2,1)} %copy.428), channel_id=1, source_target_pairs={{0,32},{32,64},{64,96},{96,128},{128,160},{160,192},{192,224},{1,3... | collective-permute-start | bytes 196616 | tf_op jit(solution)/shard_map/ppermute | solution.py:15
  80.8 10.4 %collective-permute-start.7 = (bf16[16,1,4,512]{3,0,2,1:T(8,128)(2,1)}, bf16[16,1,4,512]{3,0,2,1:T(8,128)(2,1)}, u32[]{:S(2)}, u32[]{:S(2)}) collective-permute-start(bf16[16,1,4,512]{3,0,2,1:T(8,128)(2,1)} %copy.429), channel_id=1, source_target_pairs={{32,0},{64,32},{96,64},{128,96},{160,128},{192,160},{224,192},{33,... | collective-permute-start | bytes 196616 | tf_op jit(solution)/shard_map/ppermute | solution.py:17
  92.0 16.5 %copy-start.8 = (bf16[16,6,4,512]{3,0,2,1:T(8,128)(2,1)}, bf16[16,6,4,512]{3,0,2,1:T(8,128)(2,1)S(1)}, u32[]{:S(2)}) copy-start(bf16[16,6,4,512]{3,0,2,1:T(8,128)(2,1)S(1)} %get-tuple-element.110) | copy-start | bytes 1179652
  92.8 15.7 %collective-permute-start.8 = (bf16[16,6,1,512]{3,0,2,1:T(8,128)(2,1)}, bf16[16,6,1,512]{3,0,2,1:T(8,128)(2,1)}, u32[]{:S(2)}, u32[]{:S(2)}) collective-permute-start(bf16[16,6,1,512]{3,0,2,1:T(8,128)(2,1)} %get-tuple-element.30), channel_id=1, source_target_pairs={{0,4},{4,8},{8,12},{12,16},{16,20},{20,24},{24,28},{1,5},{5,9},{9,... | collective-permute-start | bytes 294920 | tf_op jit(solution)/shard_map/ppermute | solution.py:15
  94.7 13.8 %collective-permute-start.9 = (bf16[16,6,1,512]{3,0,2,1:T(8,128)(2,1)}, bf16[16,6,1,512]{3,0,2,1:T(8,128)(2,1)S(1)}, u32[]{:S(2)}, u32[]{:S(2)}) collective-permute-start(bf16[16,6,1,512]{3,0,2,1:T(8,128)(2,1)} %get-tuple-element.31), channel_id=1, source_target_pairs={{4,0},{8,4},{12,8},{16,12},{20,16},{24,20},{28,24},{5,1},{9,5},{13... | collective-permute-start | bytes 294920 | tf_op jit(solution)/shard_map/ppermute | solution.py:17
  166.6 15.6 %copy-start.33 = (bf16[256,512]{1,0:T(8,128)(2,1)S(1)}, bf16[256,512]{1,0:T(8,128)(2,1)}, u32[]{:S(2)}) copy-start(bf16[256,512]{1,0:T(8,128)(2,1)} %reshape.377) | copy-start | bytes 786436
  167.5 14.9 %copy-start.32 = (bf16[256,512]{1,0:T(8,128)(2,1)S(1)}, bf16[256,512]{1,0:T(8,128)(2,1)}, u32[]{:S(2)}) copy-start(bf16[256,512]{1,0:T(8,128)(2,1)} %reshape.378) | copy-start | bytes 786436
  169.3 13.4 %copy-start.31 = (bf16[256,512]{1,0:T(8,128)(2,1)S(1)}, bf16[256,512]{1,0:T(8,128)(2,1)}, u32[]{:S(2)}) copy-start(bf16[256,512]{1,0:T(8,128)(2,1)} %reshape.379) | copy-start | bytes 786436
  187.7 15.4 %collective-permute-start.10 = (bf16[16,1,4,128]{3,0,2,1:T(8,128)(2,1)S(1)}, bf16[16,1,4,128]{3,0,2,1:T(8,128)(2,1)S(1)}, u32[]{:S(2)}, u32[]{:S(2)}) collective-permute-start(bf16[16,1,4,128]{3,0,2,1:T(8,128)(2,1)S(1)} %get-tuple-element.107), channel_id=1, source_target_pairs={{0,32},{32,64},{64,96},{96,128},{128,160},{160,192},{192,224},{1,3... | collective-permute-start | bytes 49160 | tf_op jit(solution)/shard_map/ppermute | solution.py:15
  194.5 9.5 %collective-permute-start.11 = (bf16[16,1,4,128]{3,0,2,1:T(8,128)(2,1)S(1)}, bf16[16,1,4,128]{3,0,2,1:T(8,128)(2,1)S(1)}, u32[]{:S(2)}, u32[]{:S(2)}) collective-permute-start(bf16[16,1,4,128]{3,0,2,1:T(8,128)(2,1)S(1)} %get-tuple-element.108), channel_id=1, source_target_pairs={{32,0},{64,32},{96,64},{128,96},{160,128},{192,160},{224,192},{33,... | collective-permute-start | bytes 49160 | tf_op jit(solution)/shard_map/ppermute | solution.py:17
  204.1 5.2 collective-permute-start.12
  207.9 5.5 collective-permute-start.13
  221.8 80.3 %reduce-scatter.4.cloned.1.call-start = ((), (), s32[]{:S(2)}) async-start(), calls=%async_computation.3 | async-start | bytes 655360 | tf_op jit(solution)/shard_map/reduce_scatter | solution.py:138
  225.2 48.8 %copy-start.64 = (bf16[8,128,512]{2,1,0:T(8,128)(2,1)S(1)}, bf16[8,128,512]{2,1,0:T(8,128)(2,1)}, u32[]{:S(2)}) copy-start(bf16[8,128,512]{2,1,0:T(8,128)(2,1)} %param.9) | copy-start | bytes 3145732
  225.2 148.4 %all-reduce.8.cloned.1.call-start = ((), (), s32[]{:S(2)}) async-start(), calls=%async_computation.4 | async-start | bytes 1769472 | tf_op jit(solution)/shard_map/psum | solution.py:165
  227.4 74.7 %copy-start.59 = (f32[512,128]{1,0:T(8,128)S(1)}, f32[512,128]{1,0:T(8,128)}, u32[]{:S(2)}) copy-start(f32[512,128]{1,0:T(8,128)} %get-tuple-element.118) | copy-start | bytes 786436
  227.4 74.7 %copy-start.62 = (bf16[8,8,8,128]{3,2,1,0:T(8,128)(2,1)S(1)}, bf16[8,8,8,128]{3,2,1,0:T(8,128)(2,1)}, u32[]{:S(2)}) copy-start(bf16[8,8,8,128]{3,2,1,0:T(8,128)(2,1)} %param.7) | copy-start | bytes 393220
  227.5 76.4 %copy-start.5 = (bf16[9,10,10,128]{3,2,1,0:T(8,128)(2,1)S(1)}, bf16[9,10,10,128]{3,2,1,0:T(8,128)(2,1)}, u32[]{:S(2)}) copy-start(bf16[9,10,10,128]{3,2,1,0:T(8,128)(2,1)} %copy-done.4) | copy-start | bytes 691204
  311.7 498.9 %reduce-scatter.6.cloned.1.call-start = ((), (), s32[]{:S(2)}) async-start(), calls=%async_computation.5 | async-start | bytes 7188480 | tf_op jit(solution)/shard_map/reduce_scatter | solution.py:145
  315.8 494.8 %copy-start.1 = (bf16[8,512,128]{2,1,0:T(8,128)(2,1)S(1)}, bf16[8,512,128]{2,1,0:T(8,128)(2,1)}, u32[]{:S(2)}) copy-start(bf16[8,512,128]{2,1,0:T(8,128)(2,1)} %param.11) | copy-start | bytes 3145732
  (54 other events, 233.5 us)
Sparse Core Ops, SparseCore 0:
  221.9 52.0 all-reduce.9
  276.7 25.4 reduce-scatter.3
  311.8 61.7 all-reduce.7
Sparse Core Ops, SparseCore 1:
  315.9 434.7 reduce-scatter.5
where the time goes:
time: 828 us; the launch traced here: 818 us
  blocking collectives  451 us (54%)
  waiting for transfers between devices  140 us (17%)
  local copies, waits for them, and re-layouts  100 us (12%)
  matrix products  52 us (6%)
  starting transfers between devices  48.4 us (6%)
  between operations  19 us (2%)
    unnamed x1, blocking collectives  436 us
    psum x1, waiting for transfers between devices, body(): lax.psum(full_term.astype(jnp.bfloat16), 'gz').astype(jnp.float32)  55.8 us
    unnamed x5, waiting for transfers between devices  44.7 us
    reshape x27, local copies, waits for them, and re-layouts, conv_forward(): window = window.reshape(count_cells, padded.shape[3])  36.5 us
    ppermute x7, starting transfers between devices, with_halo(): lax.ppermute(tail, axis, [(i, (i + 1) % count) for i in range(ends)])  34.7 us
    slice x32, local copies, waits for them, and re-layouts, conv_forward(): padded[shift_z:shift_z + size_z, shift_x:shift_x + size_x, shift_y:shift_...  31.6 us
    reduce_scatter x1, waiting for transfers between devices, body(): lax.psum_scatter(lift_features(bottle, own_up).astype(jnp.bfloat16), 'gz'...  26.7 us
    dot_general x54, matrix products, conv_weight_grad(): lax.dot_general(window, flat_gradient, (((0,), (0,)), ((), ())), preferre...  23.6 us
  transfers between devices with their start and end apart: 19, of which 8 were waited for; matrix products, arithmetic and copies ran while one was open for 7% of the time, Pallas kernels for 0%

commit v1 on v0

v1 whole, which is shorter than its diff:
```python
import jax
import jax.numpy as jnp
from jax import lax
from jax.experimental import pallas as pl
from jax.experimental.pallas import tpu as pltpu
from jax.sharding import PartitionSpec as P

BF = jnp.bfloat16
F32 = jnp.float32
MESH = pl.DeviceIdType.MESH
TAPS = 27
COPIES = 64


def matmul(left, right):
    return jnp.dot(left, right, preferred_element_type=F32)


def matmul_nt(left, right):
    return lax.dot_general(left, right, (((1,), (1,)), ((), ())), preferred_element_type=F32)


def matmul_tn(left, right):
    return lax.dot_general(left, right, (((0,), (0,)), ((), ())), preferred_element_type=F32)


def slope_of(values):
    sig = jax.nn.sigmoid(values)
    return sig * (1.0 + values * (1.0 - sig))


def selection(rows, columns, column_of):
    row = lax.broadcasted_iota(jnp.int32, (rows, 128), 0)
    lane = lax.broadcasted_iota(jnp.int32, (rows, 128), 1)
    target = column_of(row)
    blocks = [
        jnp.where(target == lane + 128 * block, 1.0, 0.0).astype(BF) for block in range(columns // 128)
    ]
    return jnp.concatenate(blocks, axis=1)


def cell_of_sub(row):
    s, k = row >> 6, row & 63
    x = 2 * (k >> 4) + ((s >> 1) & 1)
    y = 2 * ((k >> 2) & 3) + (s & 1)
    z = 2 * (k & 3) + (s >> 2)
    return x, y, z


def sub_of_cell(x, y, z):
    s = (z & 1) * 4 + (x & 1) * 2 + (y & 1)
    k = ((x >> 1) * 4 + (y >> 1)) * 4 + (z >> 1)
    return s * 64 + k


def level_kernel(
    vol_hbm, cot_hbm, wc_hbm, wd_hbm, wb_hbm, wu_hbm,
    out_ref, gb_ref, gc_ref,
    vol, cot, wc, wd, wb, wu, load_sem,
    perm_xyz, perm_sub, perm_cot, perm_back, perm_out, perm_col, perm_group, perm_brick,
    plane_z, face_y, take_y, face_x, take_x,
    padded, columns, pre, cot_sub, slope_sub, hidden_sub,
    back_out, back_in, bricks, rim_out, rim_in, coarse_pad, wide, pre_low,
    grad_pad, grad_now, gface_y, gtake_y, gface_x, gtake_x,
    bottle_out, bottle_in, part_acc, part_out, part_in, fine_grad,
    gb_all, gb_one, gb_two, gb_d3, gb_three, gb_d4, gb_four, gb_d5, gb_five,
    gc_all, gc_one, gc_two, gc_e, gc_three, gc_e2, gc_four, gc_five, gc_full,
    send_sem, recv_sem,
):
    gx, gy, gz = lax.axis_index("gx"), lax.axis_index("gy"), lax.axis_index("gz")
    py, zh = gx >> 1, gx & 1
    px, core = gy >> 1, gy & 1
    used = [0]

    def remote(src, dst, device):
        slot = used[0]
        used[0] += 1
        return pltpu.make_async_remote_copy(
            src_ref=src, dst_ref=dst, send_sem=send_sem.at[slot], recv_sem=recv_sem.at[slot],
            device_id=device, device_id_type=MESH,
        )

    def around(position, step, count):
        return lax.rem(position + step, count)

    barrier = pltpu.get_barrier_semaphore()
    partners = [{"gx": around(gx, d, 8)} for d in (1, 2, 4, 6, 7)]
    partners += [{"gy": around(gy, d, 8)} for d in (1, 2, 4, 6, 7)]
    partners += [{"gz": around(gz, d, 4)} for d in (1, 2, 3)]
    for partner in partners:
        pl.semaphore_signal(barrier, inc=1, device_id=partner, device_id_type=MESH)

    loads = [
        pltpu.make_async_copy(src, dst, load_sem.at[i])
        for i, (src, dst) in enumerate(
            ((vol_hbm, vol), (cot_hbm, cot), (wu_hbm, wu), (wc_hbm, wc), (wd_hbm, wd), (wb_hbm, wb))
        )
    ]
    for load in loads:
        load.start()

    padded[...] = jnp.zeros_like(padded)
    coarse_pad[...] = jnp.zeros_like(coarse_pad)
    grad_pad[...] = jnp.zeros_like(grad_pad)
    wide[27] = jnp.zeros((256, 512), BF)
    for tap in range(TAPS, 32):
        gc_all[tap] = jnp.zeros((4, 32, 128), BF)

    @pl.when(gx == 0)
    def _():
        bricks[gz, 0:16] = jnp.zeros((16, 512), BF)

    @pl.when(gx == 7)
    def _():
        bricks[gz, 80:96] = jnp.zeros((16, 512), BF)

    def sub_to_xyz(row):
        x, y, z = cell_of_sub(row)
        return (x * 8 + y) * 8 + z

    def sub_to_zxy(row):
        x, y, z = cell_of_sub(row)
        return (z * 8 + x) * 8 + y

    perm_xyz[...] = selection(512, 512, lambda r: ((r & 7) * 8 + (r >> 6)) * 8 + ((r >> 3) & 7))
    perm_cot[...] = selection(512, 512, sub_to_zxy)

    loads[0].wait()
    pl.semaphore_wait(barrier, len(partners))

    def exchange(axis, position, count, low_src, high_dst, high_src, low_dst):
        down = remote(low_src, high_dst, {axis: around(position, count - 1, count)})
        up = remote(high_src, low_dst, {axis: around(position, 1, count)})

        @pl.when(position > 0)
        def _():
            down.start()

        @pl.when(position < count - 1)
        def _():
            up.start()

        def finish(on_low, on_high):
            @pl.when(position > 0)
            def _():
                down.wait_send()
                up.wait_recv()
                on_low()

            @pl.when(position < count - 1)
            def _():
                up.wait_send()
                down.wait_recv()
                on_high()

        return finish

    finish_z = exchange(
        "gz", gz, 4, vol.at[pl.ds(0, 64)], plane_z.at[1], vol.at[pl.ds(448, 64)], plane_z.at[0]
    )

    loads[1].wait()
    cot_sub[...] = matmul(perm_cot[...], cot[...]).astype(BF)
    loads[2].wait()
    back = jnp.zeros((64, 512), F32)
    for s in range(8):
        back = back + matmul_nt(cot_sub[pl.ds(64 * s, 64)], wu[s])
    for q in range(4):
        back_out[q] = back[:, 128 * q : 128 * (q + 1)].astype(BF)
    back_copies = []
    for d in (1, 2, 3):
        peer = around(gz, d, 4)
        copy = remote(back_out.at[peer], back_in.at[gz], {"gz": peer})
        copy.start()
        back_copies.append(copy)
    back_in[gz] = back_out[gz]

    main = matmul(perm_xyz[...], vol[...])
    padded[1:9, 1:9, 8:16, :] = main.reshape(8, 8, 8, 128)
    flat = padded.reshape(2400, 128)

    def at_row(x, y, z):
        return (x * 10 + y) * 24 + 7 + z

    def put_plane(side, z):
        plane = plane_z[side].astype(F32)
        for x in range(8):
            flat[pl.ds(at_row(x + 1, 1, z), 8, stride=24), :] = plane[8 * x : 8 * x + 8]

    finish_z(lambda: put_plane(0, 0), lambda: put_plane(1, 9))

    for side, y in ((0, 1), (1, 8)):
        face_y[side, 0:64] = padded[1:9, y, 8:16, :].reshape(64, 128).astype(BF)
        rims = [flat[pl.ds(at_row(1, y, z), 8, stride=240), :] for z in (0, 9)]
        face_y[side, 64:80] = jnp.concatenate(rims, axis=0).astype(BF)
    finish_y = exchange("gy", gy, 8, face_y.at[0], take_y.at[1], face_y.at[1], take_y.at[0])

    perm_sub[...] = selection(512, 512, sub_to_xyz)
    perm_back[...] = selection(512, 512, lambda r: sub_of_cell(r >> 6, (r >> 3) & 7, r & 7))
    perm_out[...] = selection(512, 512, lambda r: sub_of_cell((r >> 3) & 7, r & 7, r >> 6))
    perm_col[...] = selection(384, 384, lambda r: ((r & 15) >> 2) * 96 + (r >> 4) * 4 + (r & 3))
    perm_group[...] = selection(256, 256, lambda r: ((r & 15) >> 2) * 64 + (r >> 4) * 4 + (r & 3))
    perm_brick[...] = selection(256, 256, lambda r: ((r & 63) >> 2) * 16 + (r >> 6) * 4 + (r & 3))

    def put_y(side, y):
        face = take_y[side].astype(F32)
        padded[1:9, y, 8:16, :] = face[0:64].reshape(8, 8, 128)
        for i, z in enumerate((0, 9)):
            flat[pl.ds(at_row(1, y, z), 8, stride=240), :] = face[64 + 8 * i : 72 + 8 * i]

    finish_y(lambda: put_y(0, 0), lambda: put_y(1, 9))

    for side, x in ((0, 1), (1, 8)):
        face_x[side, 0:80] = padded[x, 0:10, 8:16, :].reshape(80, 128).astype(BF)
        for i, z in enumerate((0, 9)):
            first = flat[pl.ds(at_row(x, 0, z), 8, stride=24), :]
            rest = flat[pl.ds(at_row(x, 2, z), 8, stride=24), :]
            face_x[side, 80 + 16 * i : 96 + 16 * i] = jnp.concatenate([first, rest], axis=0).astype(BF)
    finish_x = exchange("gx", gx, 8, face_x.at[0], take_x.at[1], face_x.at[1], take_x.at[0])

    def put_x(side, x):
        face = take_x[side].astype(F32)
        padded[x, 0:10, 8:16, :] = face[0:80].reshape(10, 8, 128)
        for i, z in enumerate((0, 9)):
            flat[pl.ds(at_row(x, 0, z), 8, stride=24), :] = face[80 + 16 * i : 88 + 16 * i]
            flat[pl.ds(at_row(x, 2, z), 8, stride=24), :] = face[88 + 16 * i : 96 + 16 * i]

    finish_x(lambda: put_x(0, 0), lambda: put_x(1, 9))

    loads[3].wait()
    pre[...] = jnp.zeros_like(pre)
    for a in range(3):
        @pl.loop(0, 9)
        def _(step):
            b, c = step // 3, step % 3
            tap = a * 9 + step
            window = padded[pl.ds(b, 8), pl.ds(c, 8), 7 + a : 15 + a, :].reshape(512, 128).astype(BF)
            columns[tap] = window
            pre[...] += matmul(window, wc[tap])

    high = pre[...].astype(BF)
    low = (pre[...] - high.astype(F32)).astype(BF)
    pre_sub = matmul(perm_sub[...], high) + matmul(perm_sub[...], low)
    hidden_sub[...] = jax.nn.silu(pre_sub).astype(BF)
    slope_sub[...] = slope_of(pre_sub)

    loads[4].wait()
    coarse = jnp.zeros((64, 512), F32)
    for s in range(8):
        coarse = coarse + matmul(hidden_sub[pl.ds(64 * s, 64)], wd[s])
    bricks[gz, 16:80] = coarse.astype(BF)

    finish_cx = exchange(
        "gx", gx, 8,
        bricks.at[gz, pl.ds(16, 16)], bricks.at[gz, pl.ds(80, 16)],
        bricks.at[gz, pl.ds(64, 16)], bricks.at[gz, pl.ds(0, 16)],
    )
    brick_copies = []
    for d in (1, 2, 3):
        own = bricks.at[gz, pl.ds(16, 64)]
        copy = remote(own, own, {"gz": around(gz, d, 4)})
        copy.start()
        brick_copies.append(copy)
    finish_cx(lambda: None, lambda: None)
    for d in (1, 2, 3):
        for first in (0, 80):
            rim = bricks.at[gz, pl.ds(first, 16)]
            copy = remote(rim, rim, {"gz": around(gz, d, 4)})
            copy.start()
            brick_copies.append(copy)
    for copy in back_copies:
        copy.wait()
    for copy in brick_copies:
        copy.wait()

    column = matmul(perm_col[...], bricks[...].reshape(384, 512)).reshape(6, 4, 16, 512)
    coarse_pad[0:6, 1:5, 8:24, :] = column
    for side, y in ((0, 0), (1, 3)):
        rim_out[side] = column[:, y].reshape(96, 512).astype(BF)
    finish_cy = exchange("gy", gy, 8, rim_out.at[0], rim_in.at[1], rim_out.at[1], rim_in.at[0])

    back_column = matmul(perm_group[...], back_in[...].reshape(256, 128))

    def put_rim(side, y):
        coarse_pad[0:6, y, 8:24, :] = rim_in[side].astype(F32).reshape(6, 16, 512)

    finish_cy(lambda: put_rim(0, 0), lambda: put_rim(1, 5))

    loads[5].wait()
    pre_low[...] = jnp.zeros_like(pre_low)
    for a in range(3):
        @pl.loop(0, 9)
        def _(step):
            b, c = step // 3, step % 3
            tap = a * 9 + step
            window = coarse_pad[pl.ds(b, 4), pl.ds(c, 4), 7 + a : 23 + a, :].reshape(256, 512).astype(BF)
            wide[tap] = window
            pre_low[...] += matmul(window, wb[tap])

    bottle_grad = (back_column * slope_of(pre_low[...])).astype(BF)
    grad_now[...] = bottle_grad
    grad_wide = bottle_grad.astype(F32).reshape(4, 4, 16, 128)
    grad_pad[1:5, 1:5, 8:24, :] = grad_wide
    for side, y in ((0, 0), (1, 3)):
        gface_y[side] = grad_wide[:, y].reshape(64, 128).astype(BF)
    finish_gy = exchange("gy", gy, 8, gface_y.at[0], gtake_y.at[1], gface_y.at[1], gtake_y.at[0])

    bottle = jax.nn.silu(pre_low[...]).astype(BF)
    bottle_out[...] = matmul(perm_brick[...], bottle).astype(BF).reshape(4, 64, 128)
    bottle_copies = []
    for d in (1, 2, 3):
        peer = around(gz, d, 4)
        copy = remote(bottle_out.at[peer], bottle_in.at[gz], {"gz": peer})
        copy.start()
        bottle_copies.append(copy)
    bottle_in[gz] = bottle_out[gz]

    def put_gy(side, y):
        grad_pad[1:5, y, 8:24, :] = gtake_y[side].astype(F32).reshape(4, 16, 128)

    finish_gy(lambda: put_gy(0, 0), lambda: put_gy(1, 5))
    for side, x in ((0, 1), (1, 4)):
        gface_x[side] = grad_pad[x, 0:6, 8:24, :].reshape(96, 128).astype(BF)
    finish_gx = exchange("gx", gx, 8, gface_x.at[0], gtake_x.at[1], gface_x.at[1], gtake_x.at[0])

    mine, other = core * 14, (1 - core) * 14

    def bottle_taps(first):
        @pl.loop(0, 14)
        def _(step):
            term = matmul_tn(wide[first + step], grad_now[...])
            gb_all[first + step] = term.astype(BF).reshape(4, 128, 128)

    bottle_taps(other)
    gb_first = remote(gb_all.at[pl.ds(other, 14)], gb_one, {"gy": gy ^ 1})
    gb_first.start()
    bottle_taps(mine)

    def put_gx(side, x):
        grad_pad[x, 0:6, 8:24, :] = gtake_x[side].astype(F32).reshape(6, 16, 128)

    finish_gx(lambda: put_gx(0, 0), lambda: put_gx(1, 5))

    part_acc[...] = jnp.zeros_like(part_acc)
    for a in range(3):
        @pl.loop(0, 9)
        def _(step):
            b, c = step // 3, step % 3
            window = grad_pad[pl.ds(2 - b, 4), pl.ds(2 - c, 4), 9 - a : 25 - a, :].reshape(256, 128).astype(BF)
            part_acc[...] += matmul_nt(window, wb[a * 9 + step])

    part_out[...] = matmul(perm_brick[...], part_acc[...].astype(BF)).astype(BF).reshape(4, 64, 512)
    part_copies = []
    for d in (1, 2, 3):
        peer = around(gz, d, 4)
        copy = remote(part_out.at[peer], part_in.at[d - 1], {"gz": peer})
        copy.start()
        part_copies.append(copy)

    gb_first.wait()

    @pl.loop(0, 14)
    def _(step):
        total = gb_all[mine + step].astype(F32) + gb_one[step].astype(F32)
        gb_all[mine + step] = total.astype(BF)

    gb_second = []
    for d in (1, 2, 3):
        copy = remote(
            gb_all.at[pl.ds(mine, 14), around(py, d, 4)], gb_two.at[d - 1], {"gx": around(gx, 2 * d, 8)}
        )
        copy.start()
        gb_second.append(copy)

    for copy in bottle_copies:
        copy.wait()
    for s in range(8):
        lifted = jnp.zeros((64, 128), F32)
        for q in range(4):
            lifted = lifted + matmul(bottle_in[q], wu[s, pl.ds(128 * q, 128)])
        total = lifted + hidden_sub[pl.ds(64 * s, 64)].astype(F32)
        fine_grad[pl.ds(64 * s, 64)] = total.astype(BF)
    out_ref[...] = matmul(perm_out[...], fine_grad[...]).astype(BF)

    for copy in part_copies:
        copy.wait()
    coarse_grad = part_out[gz].astype(F32)
    for d in range(3):
        coarse_grad = coarse_grad + part_in[d].astype(F32)
    coarse_grad = coarse_grad.astype(BF)
    for s in range(8):
        rows = pl.ds(64 * s, 64)
        spread = matmul_nt(coarse_grad, wd[s]) + cot_sub[rows].astype(F32)
        fine_grad[rows] = (spread * slope_sub[rows]).astype(BF)
    fine_grad[...] = matmul(perm_back[...], fine_grad[...]).astype(BF)

    def fine_taps(first, count):
        @pl.loop(0, count)
        def _(step):
            term = matmul_tn(columns[first + step], fine_grad[...])
            gc_all[first + step] = term.astype(BF).reshape(4, 32, 128)

    keep, give = core * 16, (1 - core) * 16
    fine_taps(give, 16 - 5 * (1 - core))
    gc_first = remote(gc_all.at[pl.ds(give, 16)], gc_one, {"gy": gy ^ 1})
    gc_first.start()
    fine_taps(keep, 16 - 5 * core)

    for copy in gb_second:
        copy.wait()

    @pl.loop(0, 14)
    def _(step):
        total = gb_all[mine + step, py].astype(F32)
        for d in range(3):
            total = total + gb_two[d, step].astype(F32)
        gb_d3[step] = total.astype(BF).reshape(2, 4, 16, 128)

    gc_first.wait()

    @pl.loop(0, 16)
    def _(step):
        total = gc_all[keep + step].astype(F32) + gc_one[step].astype(F32)
        gc_all[keep + step] = total.astype(BF)

    gc_second = []
    for d in (1, 2, 3):
        peer = around(px, d, 4)
        copy = remote(gc_all.at[pl.ds(keep + 4 * peer, 4)], gc_two.at[d - 1], {"gy": around(gy, 2 * d, 8)})
        copy.start()
        gc_second.append(copy)
    gb_third = []
    for d in (1, 2, 3):
        copy = remote(gb_d3.at[:, :, around(px, d, 4)], gb_three.at[d - 1], {"gy": around(gy, 2 * d, 8)})
        copy.start()
        gb_third.append(copy)

    for copy in gc_second:
        copy.wait()
    total = gc_all[pl.ds(keep + 4 * px, 4)].astype(F32)
    for d in range(3):
        total = total + gc_two[d].astype(F32)
    gc_e[...] = total.astype(BF)
    gc_third = []
    for d in (1, 2, 3):
        copy = remote(gc_e.at[:, around(py, d, 4)], gc_three.at[d - 1], {"gx": around(gx, 2 * d, 8)})
        copy.start()
        gc_third.append(copy)

    for copy in gb_third:
        copy.wait()
    total = gb_d3[:, :, px].astype(F32)
    for d in range(3):
        total = total + gb_three[d].astype(F32)
    gb_d4[...] = total.astype(BF)
    gb_fourth = remote(gb_d4.at[:, 1 - zh], gb_four, {"gx": gx ^ 1})
    gb_fourth.start()

    for copy in gc_third:
        copy.wait()
    total = gc_e[:, py].astype(F32)
    for d in range(3):
        total = total + gc_three[d].astype(F32)
    gc_e2[...] = total.astype(BF).reshape(4, 2, 16, 128)
    gc_fourth = remote(gc_e2.at[:, 1 - zh], gc_four, {"gx": gx ^ 1})
    gc_fourth.start()

    gb_fourth.wait()
    gb_d5[...] = (gb_d4[:, zh].astype(F32) + gb_four[...].astype(F32)).reshape(14, 2, 8, 128)
    gb_fifth = remote(gb_d5.at[:, 1 - core], gb_five, {"gy": gy ^ 1})
    gb_fifth.start()

    gc_fourth.wait()
    gc_five[gz] = (gc_e2[:, zh].astype(F32) + gc_four[...].astype(F32)).astype(BF)
    gc_fifth = []
    for d in (1, 2, 3):
        copy = remote(gc_five.at[gz], gc_five.at[gz], {"gz": around(gz, d, 4)})
        copy.start()
        gc_fifth.append(copy)

    gb_fifth.wait()
    gb_ref[pl.ds(mine, 14)] = gb_d5[:, core]
    gb_ref[pl.ds(other, 14)] = gb_five[...]

    for copy in gc_fifth:
        copy.wait()
    total = gc_five[0].astype(F32)
    for q in (1, 2, 3):
        total = total + gc_five[q].astype(F32)
    gc_full[core, px] = total
    gathers = []
    for d in (1, 2, 3):
        copy = remote(gc_full.at[core, px], gc_full.at[core, px], {"gy": around(gy, 2 * d, 8)})
        copy.start()
        gathers.append(copy)
    for copy in gathers:
        copy.wait()
    last = remote(gc_full.at[core], gc_full.at[core], {"gy": gy ^ 1})
    last.start()
    last.wait()
    every = gc_full[...].reshape(32, 16, 128)
    chosen = jnp.zeros((32, 2, 128), F32)
    for j in range(8):
        chosen = chosen + jnp.where(gy == j, every[:, 2 * j : 2 * j + 2, :], 0.0)
    gc_ref[...] = chosen


def body(volume, cotangent, w_conv, w_down, w_bottle, w_up):
    vmem = pltpu.VMEM
    whole = pl.BlockSpec(memory_space=pl.ANY)
    held = pl.BlockSpec(memory_space=pltpu.VMEM)
    scratch = [
        vmem((512, 128), BF), vmem((512, 128), BF), vmem((27, 128, 128), BF), vmem((8, 128, 512), BF),
        vmem((27, 512, 128), BF), vmem((8, 512, 128), BF), pltpu.SemaphoreType.DMA((6,)),
        vmem((512, 512), BF), vmem((512, 512), BF), vmem((512, 512), BF), vmem((512, 512), BF),
        vmem((512, 512), BF), vmem((384, 384), BF), vmem((256, 256), BF), vmem((256, 256), BF),
        vmem((2, 64, 128), BF), vmem((2, 80, 128), BF), vmem((2, 80, 128), BF),
        vmem((2, 112, 128), BF), vmem((2, 112, 128), BF),
        vmem((10, 10, 24, 128), F32), vmem((27, 512, 128), BF), vmem((512, 128), F32),
        vmem((512, 128), BF), vmem((512, 128), F32), vmem((512, 128), BF),
        vmem((4, 64, 128), BF), vmem((4, 64, 128), BF), vmem((4, 96, 512), BF),
        vmem((2, 96, 512), BF), vmem((2, 96, 512), BF), vmem((6, 6, 32, 512), F32),
        vmem((28, 256, 512), BF), vmem((256, 128), F32),
        vmem((6, 6, 32, 128), F32), vmem((256, 128), BF), vmem((2, 64, 128), BF), vmem((2, 64, 128), BF),
        vmem((2, 96, 128), BF), vmem((2, 96, 128), BF),
        vmem((4, 64, 128), BF), vmem((4, 64, 128), BF), vmem((256, 512), F32), vmem((4, 64, 512), BF),
        vmem((3, 64, 512), BF), vmem((512, 128), BF),
        vmem((28, 4, 128, 128), BF), vmem((14, 4, 128, 128), BF), vmem((3, 14, 128, 128), BF),
        vmem((14, 2, 4, 16, 128), BF), vmem((3, 14, 2, 16, 128), BF), vmem((14, 2, 16, 128), BF),
        vmem((14, 16, 128), BF), vmem((14, 2, 8, 128), F32), vmem((14, 8, 128), F32),
        vmem((32, 4, 32, 128), BF), vmem((16, 4, 32, 128), BF), vmem((3, 4, 4, 32, 128), BF),
        vmem((4, 4, 32, 128), BF), vmem((3, 4, 32, 128), BF), vmem((4, 2, 16, 128), BF),
        vmem((4, 16, 128), BF), vmem((4, 4, 16, 128), BF), vmem((2, 4, 4, 16, 128), F32),
        pltpu.SemaphoreType.DMA((COPIES,)), pltpu.SemaphoreType.DMA((COPIES,)),
    ]
    out, gb, gc = pl.pallas_call(
        level_kernel,
        out_shape=(
            jax.ShapeDtypeStruct((512, 128), BF),
            jax.ShapeDtypeStruct((28, 8, 128), F32),
            jax.ShapeDtypeStruct((32, 2, 128), F32),
        ),
        in_specs=[whole] * 6,
        out_specs=(held,) * 3,
        scratch_shapes=scratch,
        compiler_params=pltpu.CompilerParams(
            collective_id=0, has_side_effects=True, vmem_limit_bytes=60 * 1024 * 1024
        ),
        name="level",
    )(
        volume.reshape(512, 128),
        cotangent.reshape(512, 128),
        jnp.transpose(w_conv, (1, 0, 2)),
        w_down,
        jnp.transpose(w_bottle, (1, 0, 2)),
        w_up,
    )
    return (
        out.reshape(volume.shape),
        jnp.transpose(gc[:TAPS], (1, 0, 2)),
        jnp.transpose(gb[:TAPS], (1, 0, 2)),
    )


def solution(mesh):
    in_specs = (
        P("gz", "gx", "gy", None),
        P("gz", "gx", "gy", None),
        P(),
        P(),
        P(None, None, "gz"),
        P(),
    )
    out_specs = (
        P("gz", "gx", "gy", None),
        P(("gx", "gy"), None, None),
        P(("gx", "gy"), None, "gz"),
    )
    return jax.shard_map(body, mesh=mesh, in_specs=in_specs, out_specs=out_specs, check_vma=False)
```

time: 828 us -> 124 us (0.15)
  the two profiles are of different devices: /device:TPU:0 before, /device:TPU:1 now
where the time goes in v1:
time: 124 us
  Pallas kernels  118 us (95%)
  local copies, waits for them, and re-layouts  4.47 us (4%)
    pallas_call x1, Pallas kernels, body(): pl.pallas_call(level_kernel, out_shape=(jax.ShapeDtypeStruct((512, 128),...  118 us

profile of v1, /device:TPU:1, one launch (start us, length us, event | category | flops | bytes accessed | tf_op | source)
XLA Modules:
  0.0 123.5 jit_solution(9656298770558119578)
XLA Ops:
  0.6 118.4 %level.1 = (bf16[512,128]{1,0:T(8,128)(2,1)}, f32[28,8,128]{2,1,0:T(8,128)}, f32[32,2,128]{2,1,0:T(2,128)}) custom-call(bf16[512,128]{1,0:T(8,128)(2,1)} %bitcast.11, bf16[512,128]{1,0:T(8,128)(2,1)} %bitcast.12, bf16[27,128,128]{2,1,0:T(8,128)(2,1)} %bitcast.10, bf16[8,128,512]{2,1,0:T(8,128)(2,1)} %wd_hbm.1, bf16[27,512,128]{2,1,0:T(8,128)(2,1)} %bitcast.9, ...), custom_call_target="tpu_custom_call" | custom-call | tf_op jit(solution)/shard_map/level/pallas_call | solution.py:536
  119.0 1.4 %slice_bitcast_fusion.1 = f32[2,27,128]{2,0,1:T(2,128)} fusion(f32[32,2,128]{2,1,0:T(2,128)} %get-tuple-element.7), kind=kLoop, calls=%fused_computation.1 | loop fusion | bytes 55296 | tf_op jit(solution)/shard_map/transpose | solution.py:560
  120.4 1.5 %slice_bitcast_fusion = f32[8,27,128]{2,0,1:T(8,128)} fusion(f32[28,8,128]{2,1,0:T(8,128)} %get-tuple-element.8), kind=kLoop, calls=%fused_computation | loop fusion | bytes 221184 | tf_op jit(solution)/shard_map/transpose | solution.py:561
  121.9 1.6 %copy.10 = bf16[8,8,8,128]{3,2,1,0:T(8,128)(2,1)} copy(bf16[8,8,8,128]{3,2,1,0:T(8,128)(2,1)} %bitcast.13) | data formatting | bytes 262144

commit v2 on v1

v2 whole, which is shorter than its diff:
```python
import jax
import jax.numpy as jnp
from jax import lax
from jax.experimental import pallas as pl
from jax.experimental.pallas import tpu as pltpu
from jax.sharding import PartitionSpec as P

BF = jnp.bfloat16
F32 = jnp.float32
MESH = pl.DeviceIdType.MESH
TAPS = 27
COPIES = 96


def matmul(left, right):
    return jnp.dot(left, right, preferred_element_type=F32)


def matmul_nt(left, right):
    return lax.dot_general(left, right, (((1,), (1,)), ((), ())), preferred_element_type=F32)


def matmul_tn(left, right):
    return lax.dot_general(left, right, (((0,), (0,)), ((), ())), preferred_element_type=F32)


def slope_of(values):
    sig = jax.nn.sigmoid(values)
    return sig * (1.0 + values * (1.0 - sig))


def selection(rows, columns, column_of):
    row = lax.broadcasted_iota(jnp.int32, (rows, 128), 0)
    lane = lax.broadcasted_iota(jnp.int32, (rows, 128), 1)
    target = column_of(row)
    blocks = [
        jnp.where(target == lane + 128 * block, 1.0, 0.0).astype(BF) for block in range(columns // 128)
    ]
    return jnp.concatenate(blocks, axis=1)


def cell_of_sub(row):
    s, k = row >> 6, row & 63
    x = 2 * (k >> 4) + ((s >> 1) & 1)
    y = 2 * ((k >> 2) & 3) + (s & 1)
    z = 2 * (k & 3) + (s >> 2)
    return x, y, z


def sub_of_cell(x, y, z):
    s = (z & 1) * 4 + (x & 1) * 2 + (y & 1)
    k = ((x >> 1) * 4 + (y >> 1)) * 4 + (z >> 1)
    return s * 64 + k


def level_kernel(
    vol_hbm, cot_hbm, wc_hbm, wd_hbm, wb_hbm, wu_hbm,
    out_ref, gb_ref, gc_ref,
    vol, cot, wc, wd, wb, wu, load_sem,
    perm_xyz, perm_sub, perm_cot, perm_back, perm_out, perm_group, perm_rim, perm_brick, lift_z,
    plane_z, face_y, take_y, face_x, take_x,
    padded, columns, turned, pre, cot_sub, slope_sub, hidden_sub,
    back_out, back_in, bricks, rims, shifted, rim_out, rim_in, corner_out, corner_in, pre_low,
    grad_now, grad_shift, gface_y, gtake_y, gface_x, gtake_x,
    bottle_out, bottle_in, part_acc, part_out, part_in, fine_grad,
    gb_all, gb_one, gb_ya, gb_xb, gb_a, gb_b, gb_xa, gb_yb, gb_d4, gb_four, gb_d5, gb_five, gb_rows,
    gc_all, gc_one, gc_xa, gc_yb, gc_a, gc_b, gc_ya, gc_xb, gc_e2, gc_z, gc_half, gc_g,
    send_sem, recv_sem,
):
    gx, gy, gz = lax.axis_index("gx"), lax.axis_index("gy"), lax.axis_index("gz")
    py, zh = gx >> 1, gx & 1
    px, core = gy >> 1, gy & 1
    used = [0]

    def remote(src, dst, device):
        slot = used[0]
        used[0] += 1
        return pltpu.make_async_remote_copy(
            src_ref=src, dst_ref=dst, send_sem=send_sem.at[slot], recv_sem=recv_sem.at[slot],
            device_id=device, device_id_type=MESH,
        )

    def around(position, step, count):
        return lax.rem(position + step, count)

    barrier = pltpu.get_barrier_semaphore()
    partners = [{"gx": around(gx, d, 8)} for d in (1, 2, 4, 6, 7)]
    partners += [{"gy": around(gy, d, 8)} for d in range(1, 8)]
    partners += [{"gz": around(gz, d, 4)} for d in (1, 2, 3)]
    partners += [{"gx": gx ^ 1, "gz": around(gz, d, 4)} for d in (1, 2, 3)]
    for partner in partners:
        pl.semaphore_signal(barrier, inc=1, device_id=partner, device_id_type=MESH)

    loads = [
        pltpu.make_async_copy(src, dst, load_sem.at[i])
        for i, (src, dst) in enumerate(
            ((vol_hbm, vol), (cot_hbm, cot), (wu_hbm, wu), (wc_hbm, wc), (wd_hbm, wd), (wb_hbm, wb))
        )
    ]
    for load in loads:
        load.start()

    padded[...] = jnp.zeros_like(padded)
    for side in (0, 5):
        for a in range(3):
            shifted[a, side] = jnp.zeros((6, 16, 512), BF)
            grad_shift[a, side] = jnp.zeros((6, 16, 128), BF)
    for tap in range(TAPS, 32):
        gc_all[tap] = jnp.zeros((4, 32, 128), BF)
    gb_all[27] = jnp.zeros((4, 2, 4, 16, 128), BF)
    corner_in[2:4] = jnp.zeros((2, 32, 512), BF)
    for side in range(2):
        gtake_x[side, 96:128] = jnp.zeros((32, 128), BF)

    for side, edge in ((0, 0), (1, 7)):
        @pl.when(gx == edge)
        def _():
            rims[gz, 16 * side : 16 * side + 16] = jnp.zeros((16, 512), BF)
            gtake_x[side, 0:96] = jnp.zeros((96, 128), BF)

        @pl.when(gy == edge)
        def _():
            rim_in[side] = jnp.zeros((64, 512), BF)
            corner_in[side] = jnp.zeros((32, 512), BF)
            gtake_y[side] = jnp.zeros((64, 128), BF)

    def sub_to_xyz(row):
        x, y, z = cell_of_sub(row)
        return (x * 8 + y) * 8 + z

    def sub_to_zxy(row):
        x, y, z = cell_of_sub(row)
        return (z * 8 + x) * 8 + y

    perm_xyz[...] = selection(512, 512, lambda r: ((r & 7) * 8 + (r >> 6)) * 8 + ((r >> 3) & 7))
    perm_cot[...] = selection(512, 512, sub_to_zxy)

    loads[0].wait()
    pl.semaphore_wait(barrier, len(partners))

    def exchange(axis, position, count, low_src, high_dst, high_src, low_dst):
        down = remote(low_src, high_dst, {axis: around(position, count - 1, count)})
        up = remote(high_src, low_dst, {axis: around(position, 1, count)})

        @pl.when(position > 0)
        def _():
            down.start()

        @pl.when(position < count - 1)
        def _():
            up.start()

        def finish(on_low, on_high):
            @pl.when(position > 0)
            def _():
                down.wait_send()
                up.wait_recv()
                on_low()

            @pl.when(position < count - 1)
            def _():
                up.wait_send()
                down.wait_recv()
                on_high()

        return finish

    finish_z = exchange(
        "gz", gz, 4, vol.at[pl.ds(0, 64)], plane_z.at[1], vol.at[pl.ds(448, 64)], plane_z.at[0]
    )

    loads[1].wait()
    cot_sub[...] = matmul(perm_cot[...], cot[...]).astype(BF)
    loads[2].wait()
    back = jnp.zeros((64, 512), F32)
    for s in range(8):
        back = back + matmul_nt(cot_sub[pl.ds(64 * s, 64)], wu[s])
    for q in range(4):
        back_out[q] = back[:, 128 * q : 128 * (q + 1)].astype(BF)
    back_copies = []
    for d in (1, 2, 3):
        peer = around(gz, d, 4)
        copy = remote(back_out.at[peer], back_in.at[gz], {"gz": peer})
        copy.start()
        back_copies.append(copy)
    back_in[gz] = back_out[gz]

    main = matmul(perm_xyz[...], vol[...])
    padded[1:9, 1:9, 8:16, :] = main.reshape(8, 8, 8, 128)
    flat = padded.reshape(2400, 128)

    def at_row(x, y, z):
        return (x * 10 + y) * 24 + 7 + z

    def put_plane(side, z):
        plane = plane_z[side].astype(F32)
        for x in range(8):
            flat[pl.ds(at_row(x + 1, 1, z), 8, stride=24), :] = plane[8 * x : 8 * x + 8]

    finish_z(lambda: put_plane(0, 0), lambda: put_plane(1, 9))

    for side, y in ((0, 1), (1, 8)):
        face_y[side, 0:64] = padded[1:9, y, 8:16, :].reshape(64, 128).astype(BF)
        edges = [flat[pl.ds(at_row(1, y, z), 8, stride=240), :] for z in (0, 9)]
        face_y[side, 64:80] = jnp.concatenate(edges, axis=0).astype(BF)
    finish_y = exchange("gy", gy, 8, face_y.at[0], take_y.at[1], face_y.at[1], take_y.at[0])

    perm_sub[...] = selection(512, 512, sub_to_xyz)
    perm_back[...] = selection(512, 512, lambda r: sub_of_cell(r >> 6, (r >> 3) & 7, r & 7))
    perm_out[...] = selection(512, 512, lambda r: sub_of_cell((r >> 3) & 7, r & 7, r >> 6))

    def shifted_z(r, shift, column_of):
        z = (r & 15) + shift
        return jnp.where((z < 0) | (z > 15), -1, column_of(r, z & 15))

    for a in range(3):
        perm_group[a] = selection(
            256, 256, lambda r: shifted_z(r, a - 1, lambda r, z: (z >> 2) * 64 + (r >> 4) * 4 + (z & 3))
        )
        perm_rim[a] = selection(
            128, 128, lambda r: shifted_z(r, a - 1, lambda r, z: (z >> 2) * 32 + (r >> 4) * 4 + (z & 3))
        )
        lift_z[a] = selection(128, 128, lambda r: shifted_z(r, a - 1, lambda r, z: r - (r & 15) + z))
    perm_brick[...] = selection(256, 256, lambda r: ((r & 63) >> 2) * 16 + (r >> 6) * 4 + (r & 3))

    def put_y(side, y):
        face = take_y[side].astype(F32)
        padded[1:9, y, 8:16, :] = face[0:64].reshape(8, 8, 128)
        for i, z in enumerate((0, 9)):
            flat[pl.ds(at_row(1, y, z), 8, stride=240), :] = face[64 + 8 * i : 72 + 8 * i]

    finish_y(lambda: put_y(0, 0), lambda: put_y(1, 9))

    for side, x in ((0, 1), (1, 8)):
        face_x[side, 0:80] = padded[x, 0:10, 8:16, :].reshape(80, 128).astype(BF)
        for i, z in enumerate((0, 9)):
            first = flat[pl.ds(at_row(x, 0, z), 8, stride=24), :]
            rest = flat[pl.ds(at_row(x, 2, z), 8, stride=24), :]
            face_x[side, 80 + 16 * i : 96 + 16 * i] = jnp.concatenate([first, rest], axis=0).astype(BF)
    finish_x = exchange("gx", gx, 8, face_x.at[0], take_x.at[1], face_x.at[1], take_x.at[0])

    def put_x(side, x):
        face = take_x[side].astype(F32)
        padded[x, 0:10, 8:16, :] = face[0:80].reshape(10, 8, 128)
        for i, z in enumerate((0, 9)):
            flat[pl.ds(at_row(x, 0, z), 8, stride=24), :] = face[80 + 16 * i : 88 + 16 * i]
            flat[pl.ds(at_row(x, 2, z), 8, stride=24), :] = face[88 + 16 * i : 96 + 16 * i]

    finish_x(lambda: put_x(0, 0), lambda: put_x(1, 9))

    loads[3].wait()
    pre[...] = jnp.zeros_like(pre)

    @pl.loop(0, 9)
    def _(step):
        b, c = step // 3, step % 3
        windows = [
            padded[pl.ds(b, 8), pl.ds(c, 8), 7 + a : 15 + a, :].reshape(512, 128).astype(BF) for a in range(3)
        ]
        for a in range(3):
            columns[a * 9 + step] = windows[a]
        weights = jnp.concatenate([wc[a * 9 + step] for a in range(3)], axis=0)
        pre[...] += matmul(jnp.concatenate(windows, axis=1), weights)

    high = pre[...].astype(BF)
    low = (pre[...] - high.astype(F32)).astype(BF)
    pre_sub = matmul(perm_sub[...], high) + matmul(perm_sub[...], low)
    hidden_sub[...] = jax.nn.silu(pre_sub).astype(BF)
    slope_sub[...] = slope_of(pre_sub)

    loads[4].wait()
    coarse = jnp.zeros((64, 512), F32)
    for s in range(8):
        coarse = coarse + matmul(hidden_sub[pl.ds(64 * s, 64)], wd[s])
    bricks[gz] = coarse.astype(BF)

    finish_cx = exchange(
        "gx", gx, 8,
        bricks.at[gz, pl.ds(0, 16)], rims.at[gz, pl.ds(16, 16)],
        bricks.at[gz, pl.ds(48, 16)], rims.at[gz, pl.ds(0, 16)],
    )

    def send_column(ref):
        copies = []
        for d in (1, 2, 3):
            copy = remote(ref.at[gz], ref.at[gz], {"gz": around(gz, d, 4)})
            copy.start()
            copies.append(copy)
        return copies

    brick_copies = send_column(bricks)

    def turn(first, last):
        @pl.loop(first, last)
        def _(tap):
            turned[tap] = columns[tap].T

    turn(0, 16)
    finish_cx(lambda: None, lambda: None)
    rim_copies = send_column(rims)
    turn(16, 27)

    for copy in brick_copies:
        copy.wait()
    stack = bricks[...].reshape(256, 512)
    middle = matmul(perm_group[1], stack).astype(BF).reshape(4, 4, 16, 512)
    for side, y in ((0, 0), (1, 3)):
        rim_out[side] = middle[:, y].reshape(64, 512)
    finish_cy = exchange("gy", gy, 8, rim_out.at[0], rim_in.at[1], rim_out.at[1], rim_in.at[0])
    shifted[1, 1:5, 1:5] = middle
    for a in (0, 2):
        shifted[a, 1:5, 1:5] = matmul(perm_group[a], stack).astype(BF).reshape(4, 4, 16, 512)
    for copy in back_copies:
        copy.wait()
    back_column = matmul(perm_group[1], back_in[...].reshape(256, 128))

    loads[5].wait()
    finish_cy(lambda: None, lambda: None)
    for a in range(3):
        sides = matmul(lift_z[a], rim_in[...].reshape(128, 512)).astype(BF).reshape(2, 4, 16, 512)
        shifted[a, 1:5, 0] = sides[0]
        shifted[a, 1:5, 5] = sides[1]

    pre_low[...] = jnp.zeros_like(pre_low)

    def low_taps(first, last):
        @pl.loop(first, last)
        def _(step):
            b, c = step // 3, step % 3
            total = pre_low[...]
            for a in range(3):
                window = shifted[a, pl.ds(b, 4), pl.ds(c, 4)].reshape(256, 512)
                total = total + matmul(window, wb[a * 9 + step])
            pre_low[...] = total

    low_taps(0, 6)
    for copy in rim_copies:
        copy.wait()
    rim_rows = []
    for a in range(3):
        rim_rows.append(matmul(perm_rim[a], rims[...].reshape(128, 512)).astype(BF).reshape(2, 4, 16, 512))
    for side, y in ((0, 0), (1, 3)):
        corner_out[side] = rim_rows[1][:, y].reshape(32, 512)
    finish_cc = exchange("gy", gy, 8, corner_out.at[0], corner_in.at[1], corner_out.at[1], corner_in.at[0])
    low_taps(6, 9)
    for a in range(3):
        shifted[a, 0, 1:5] = rim_rows[a][0]
        shifted[a, 5, 1:5] = rim_rows[a][1]
    finish_cc(lambda: None, lambda: None)
    for a in range(3):
        corners = matmul(lift_z[a], corner_in[...].reshape(128, 512)).astype(BF).reshape(4, 2, 16, 512)
        for i, y in ((0, 0), (1, 5)):
            shifted[a, 0, y] = corners[i, 0]
            shifted[a, 5, y] = corners[i, 1]

    @pl.loop(0, 3)
    def _(c):
        low, high = pre_low[0:64], pre_low[192:256]
        for a in range(3):
            low = low + matmul(shifted[a, 0, pl.ds(c, 4)].reshape(64, 512), wb[a * 9 + c])
            high = high + matmul(shifted[a, 5, pl.ds(c, 4)].reshape(64, 512), wb[a * 9 + 6 + c])
        pre_low[0:64] = low
        pre_low[192:256] = high

    bottle_grad = (back_column * slope_of(pre_low[...])).astype(BF)
    grad_now[...] = bottle_grad
    middle = bottle_grad.astype(F32).reshape(4, 4, 16, 128)
    for side, y in ((0, 0), (1, 3)):
        gface_y[side] = middle[:, y].reshape(64, 128).astype(BF)
    finish_gy = exchange("gy", gy, 8, gface_y.at[0], gtake_y.at[1], gface_y.at[1], gtake_y.at[0])

    bottle = jax.nn.silu(pre_low[...]).astype(BF)
    bottle_out[...] = matmul(perm_brick[...], bottle).astype(BF).reshape(4, 64, 128)
    bottle_copies = []
    for d in (1, 2, 3):
        peer = around(gz, d, 4)
        copy = remote(bottle_out.at[peer], bottle_in.at[gz], {"gz": peer})
        copy.start()
        bottle_copies.append(copy)
    bottle_in[gz] = bottle_out[gz]

    for a in range(3):
        for half in range(2):
            moved = matmul(lift_z[a], grad_now[pl.ds(128 * half, 128)]).astype(BF)
            grad_shift[a, 1 + 2 * half : 3 + 2 * half, 1:5] = moved.reshape(2, 4, 16, 128)

    mine, other = core * 14, (1 - core) * 14

    def bottle_taps(first, last, base):
        @pl.loop(first, last)
        def _(step):
            tap = base + step
            depth, across = tap // 9, tap % 9
            b, c = across // 3, across % 3
            window = shifted[depth, pl.ds(b, 4), pl.ds(c, 4)].reshape(256, 512)
            gb_all[tap] = matmul_tn(window, grad_now[...]).astype(BF).reshape(4, 2, 4, 16, 128)

    bottle_taps(0, 8, other)
    finish_gy(lambda: None, lambda: None)
    for a in range(3):
        sides = matmul(lift_z[a], gtake_y[...].reshape(128, 128)).astype(BF).reshape(2, 4, 16, 128)
        grad_shift[a, 1:5, 0] = sides[0]
        grad_shift[a, 1:5, 5] = sides[1]
    for side, x in ((0, 1), (1, 4)):
        gface_x[side] = grad_shift[1, x].reshape(96, 128)
    finish_gx = exchange(
        "gx", gx, 8,
        gface_x.at[0], gtake_x.at[1, pl.ds(0, 96)], gface_x.at[1], gtake_x.at[0, pl.ds(0, 96)],
    )

    part_acc[...] = jnp.zeros_like(part_acc)

    @pl.loop(0, 9)
    def _(step):
        b, c = step // 3, step % 3
        windows = [grad_shift[2 - a, pl.ds(2 - b, 4), pl.ds(2 - c, 4)].reshape(256, 128) for a in range(3)]
        weights = jnp.concatenate([wb[a * 9 + step] for a in range(3)], axis=1)
        part_acc[...] += matmul_nt(jnp.concatenate(windows, axis=1), weights)

    finish_gx(lambda: None, lambda: None)
    for a in range(3):
        for side, x in ((0, 0), (1, 5)):
            moved = matmul(lift_z[a], gtake_x[side]).astype(BF)
            grad_shift[a, x] = moved[0:96].reshape(6, 16, 128)

    @pl.loop(0, 3)
    def _(c):
        for x, rows, b in ((0, 0, 2), (5, 192, 0)):
            windows = [grad_shift[2 - a, x, pl.ds(2 - c, 4)].reshape(64, 128) for a in range(3)]
            weights = jnp.concatenate([wb[a * 9 + 3 * b + c] for a in range(3)], axis=1)
            part_acc[rows : rows + 64] += matmul_nt(jnp.concatenate(windows, axis=1), weights)

    part_out[...] = matmul(perm_brick[...], part_acc[...].astype(BF)).astype(BF).reshape(4, 64, 512)
    part_copies = []
    for d in (1, 2, 3):
        peer = around(gz, d, 4)
        copy = remote(part_out.at[peer], part_in.at[d - 1], {"gz": peer})
        copy.start()
        part_copies.append(copy)

    bottle_taps(8, 13 + core, other)
    gb_first = remote(gb_all.at[pl.ds(other, 14)], gb_one, {"gy": gy ^ 1})
    gb_first.start()
    bottle_taps(0, 14 - core, mine)

    for copy in bottle_copies:
        copy.wait()
    for s in range(8):
        lifted = jnp.zeros((64, 128), F32)
        for q in range(4):
            lifted = lifted + matmul(bottle_in[q], wu[s, pl.ds(128 * q, 128)])
        total = lifted + hidden_sub[pl.ds(64 * s, 64)].astype(F32)
        fine_grad[pl.ds(64 * s, 64)] = total.astype(BF)
    out_ref[...] = matmul(perm_out[...], fine_grad[...]).astype(BF)

    gb_first.wait()

    @pl.loop(0, 14)
    def _(step):
        total = gb_all[mine + step].astype(F32) + gb_one[step].astype(F32)
        gb_all[mine + step] = total.astype(BF)

    def along_y(source_of, target):
        copies = []
        for d in (1, 2, 3):
            copy = remote(source_of(around(py, d, 4)), target.at[d - 1], {"gx": around(gx, 2 * d, 8)})
            copy.start()
            copies.append(copy)
        return copies

    def along_x(source_of, target):
        copies = []
        for d in (1, 2, 3):
            copy = remote(source_of(around(px, d, 4)), target.at[d - 1], {"gy": around(gy, 2 * d, 8)})
            copy.start()
            copies.append(copy)
        return copies

    gb_second = along_y(lambda y: gb_all.at[pl.ds(mine, 7), y], gb_ya)
    gb_second += along_x(lambda x: gb_all.at[pl.ds(mine + 7, 7), :, :, x], gb_xb)

    for copy in part_copies:
        copy.wait()
    coarse_grad = part_out[gz].astype(F32)
    for d in range(3):
        coarse_grad = coarse_grad + part_in[d].astype(F32)
    coarse_grad = coarse_grad.astype(BF)
    for s in range(8):
        rows = pl.ds(64 * s, 64)
        spread = matmul_nt(coarse_grad, wd[s]) + cot_sub[rows].astype(F32)
        fine_grad[rows] = (spread * slope_sub[rows]).astype(BF)
    fine_grad[...] = matmul(perm_back[...], fine_grad[...]).astype(BF)

    def fine_taps(first, last, base):
        @pl.loop(first, last)
        def _(step):
            term = matmul(turned[base + step], fine_grad[...])
            gc_all[base + step] = term.astype(BF).reshape(4, 32, 128)

    keep, give = core * 16, (1 - core) * 16
    fine_taps(0, 16 - 5 * (1 - core), give)
    gc_first = remote(gc_all.at[pl.ds(give, 16)], gc_one, {"gy": gy ^ 1})
    gc_first.start()
    fine_taps(0, 16 - 5 * core, keep)

    gc_first.wait()

    @pl.loop(0, 16)
    def _(step):
        total = gc_all[keep + step].astype(F32) + gc_one[step].astype(F32)
        gc_all[keep + step] = total.astype(BF)

    gc_second = along_x(lambda x: gc_all.at[pl.ds(keep + 2 * x, 2)], gc_xa)
    gc_second += along_y(lambda y: gc_all.at[pl.ds(keep + 8, 8), y], gc_yb)

    def summed(own, taken):
        total = own.astype(F32)
        for d in range(3):
            total = total + taken[d].astype(F32)
        return total

    for copy in gb_second:
        copy.wait()

    @pl.loop(0, 7)
    def _(step):
        total = gb_all[mine + step, py].astype(F32)
        other_half = gb_all[mine + 7 + step, :, :, px].astype(F32)
        for d in range(3):
            total = total + gb_ya[d, step].astype(F32)
            other_half = other_half + gb_xb[d, step].astype(F32)
        gb_a[step] = total.astype(BF)
        gb_b[step] = other_half.astype(BF)

    gb_third = along_x(lambda x: gb_a.at[:, :, x], gb_xa)
    gb_third += along_y(lambda y: gb_b.at[:, y], gb_yb)

    for copy in gc_second:
        copy.wait()
    gc_a[...] = summed(gc_all[pl.ds(keep + 2 * px, 2)], gc_xa).astype(BF)
    gc_b[...] = summed(gc_all[pl.ds(keep + 8, 8), py], gc_yb).astype(BF)
    gc_third = along_y(lambda y: gc_a.at[:, y], gc_ya)
    gc_third += along_x(lambda x: gc_b.at[pl.ds(2 * x, 2)], gc_xb)

    for copy in gb_third:
        copy.wait()
    gb_d4[0:7] = summed(gb_a[:, :, px], gb_xa).astype(BF)
    gb_d4[7:14] = summed(gb_b[:, py], gb_yb).astype(BF)
    gb_fourth = remote(gb_d4.at[:, 1 - zh], gb_four, {"gx": gx ^ 1})
    gb_fourth.start()

    for copy in gc_third:
        copy.wait()
    gc_e2[0:2] = summed(gc_a[:, py], gc_ya).astype(BF).reshape(2, 2, 16, 128)
    gc_e2[2:4] = summed(gc_b[pl.ds(2 * px, 2)], gc_xb).astype(BF).reshape(2, 2, 16, 128)
    slot = zh * 4 + gz
    gc_fourth = []
    for d in range(4):
        peer = around(gz, d, 4)
        copy = remote(gc_e2.at[:, 1 - zh], gc_z.at[slot], {"gx": gx ^ 1, "gz": peer})
        copy.start()
        gc_fourth.append(copy)
        if d > 0:
            copy = remote(gc_e2.at[:, zh], gc_z.at[slot], {"gz": peer})
            copy.start()
            gc_fourth.append(copy)
    gc_z[slot] = gc_e2[:, zh]

    gb_fourth.wait()
    gb_d5[...] = (gb_d4[:, zh].astype(F32) + gb_four[...].astype(F32)).reshape(14, 2, 8, 128)
    gb_fifth = remote(gb_d5.at[:, 1 - core], gb_five, {"gy": gy ^ 1})
    gb_fifth.start()

    for copy in gc_fourth:
        copy.wait()
    total = gc_z[0].astype(F32)
    for q in range(1, 8):
        total = total + gc_z[q].astype(F32)
    for half in range(2):
        gc_half[half] = total[:, 8 * half : 8 * half + 8]
    gathers = []
    for d in range(1, 8):
        peer = around(gy, d, 8)
        copy = remote(gc_half.at[peer >> 2], gc_g.at[gy], {"gy": peer})
        copy.start()
        gathers.append(copy)
    gc_g[gy] = gc_half[gy >> 2]

    gb_fifth.wait()
    for step in range(14):
        gb_rows[pl.ds(mine + step, 8, stride=32), :] = gb_d5[step, core]
        gb_rows[pl.ds(other + step, 8, stride=32), :] = gb_five[step]
    gb_ref[...] = gb_rows[...].reshape(8, 32, 128)[:, 0:TAPS]

    for copy in gathers:
        copy.wait()
    place = gy & 3
    for source in range(8):
        block = gc_g[source]
        chosen = jnp.zeros((4, 2, 128), F32)
        for j in range(4):
            chosen = chosen + jnp.where(place == j, block[:, 2 * j : 2 * j + 2, :], 0.0)
        first = (source & 1) * 16 + (source >> 1) * 2
        gc_ref[first : first + 2] = chosen[0:2]
        gc_ref[first + 8 : first + 10] = chosen[2:4]


def deliver_kernel(out_ref, gb_ref, out_final, gb_final):
    out_final[...] = out_ref[...]
    gb_final[...] = gb_ref[...]


def body(volume, cotangent, w_conv, w_down, w_bottle, w_up):
    vmem = pltpu.VMEM
    whole = pl.BlockSpec(memory_space=pl.ANY)
    held = pl.BlockSpec(memory_space=pltpu.VMEM)
    def kept(*shape):
        return vmem(shape, BF)

    scratch = [
        kept(512, 128), kept(512, 128), kept(27, 128, 128), kept(8, 128, 512),
        kept(27, 512, 128), kept(8, 512, 128), pltpu.SemaphoreType.DMA((6,)),
        kept(512, 512), kept(512, 512), kept(512, 512), kept(512, 512), kept(512, 512),
        kept(3, 256, 256), kept(3, 128, 128), kept(256, 256), kept(3, 128, 128),
        kept(2, 64, 128), kept(2, 80, 128), kept(2, 80, 128), kept(2, 112, 128), kept(2, 112, 128),
        vmem((10, 10, 24, 128), F32), kept(27, 512, 128), kept(27, 128, 512), vmem((512, 128), F32),
        kept(512, 128), vmem((512, 128), F32), kept(512, 128),
        kept(4, 64, 128), kept(4, 64, 128), kept(4, 64, 512), kept(4, 32, 512), kept(3, 6, 6, 16, 512),
        kept(2, 64, 512), kept(2, 64, 512), kept(2, 32, 512), kept(4, 32, 512), vmem((256, 128), F32),
        kept(256, 128), kept(3, 6, 6, 16, 128), kept(2, 64, 128), kept(2, 64, 128),
        kept(2, 96, 128), kept(2, 128, 128),
        kept(4, 64, 128), kept(4, 64, 128), vmem((256, 512), F32), kept(4, 64, 512),
        kept(3, 64, 512), kept(512, 128),
        kept(28, 4, 2, 4, 16, 128), kept(14, 4, 2, 4, 16, 128), kept(3, 7, 2, 4, 16, 128), kept(3, 7, 4, 2, 16, 128),
        kept(7, 2, 4, 16, 128), kept(7, 4, 2, 16, 128), kept(3, 7, 2, 16, 128), kept(3, 7, 2, 16, 128),
        kept(14, 2, 16, 128), kept(14, 16, 128), vmem((14, 2, 8, 128), F32), vmem((14, 8, 128), F32),
        vmem((256, 128), F32),
        kept(32, 4, 32, 128), kept(16, 4, 32, 128), kept(3, 2, 4, 32, 128), kept(3, 8, 32, 128),
        kept(2, 4, 32, 128), kept(8, 32, 128), kept(3, 2, 32, 128), kept(3, 2, 32, 128),
        kept(4, 2, 16, 128), kept(8, 4, 16, 128), vmem((2, 4, 8, 128), F32), vmem((8, 4, 8, 128), F32),
        pltpu.SemaphoreType.DMA((COPIES,)), pltpu.SemaphoreType.DMA((COPIES,)),
    ]
    out, gb, gc = pl.pallas_call(
        level_kernel,
        out_shape=(
            jax.ShapeDtypeStruct((512, 128), BF),
            jax.ShapeDtypeStruct((8, TAPS, 128), F32),
            jax.ShapeDtypeStruct((32, 2, 128), F32),
        ),
        in_specs=[whole] * 6,
        out_specs=(held,) * 3,
        scratch_shapes=scratch,
        compiler_params=pltpu.CompilerParams(
            collective_id=0, has_side_effects=True, vmem_limit_bytes=60 * 1024 * 1024
        ),
        name="level",
    )(
        volume.reshape(512, 128),
        cotangent.reshape(512, 128),
        jnp.transpose(w_conv, (1, 0, 2)),
        w_down,
        jnp.transpose(w_bottle, (1, 0, 2)),
        w_up,
    )
    out, gb = pl.pallas_call(
        deliver_kernel,
        out_shape=(jax.ShapeDtypeStruct(out.shape, BF), jax.ShapeDtypeStruct(gb.shape, F32)),
        in_specs=[held] * 2,
        out_specs=(held,) * 2,
        name="deliver",
    )(out, gb)
    return out.reshape(volume.shape), jnp.transpose(gc[:TAPS], (1, 0, 2)), gb


def solution(mesh):
    in_specs = (
        P("gz", "gx", "gy", None),
        P("gz", "gx", "gy", None),
        P(),
        P(),
        P(None, None, "gz"),
        P(),
    )
    out_specs = (
        P("gz", "gx", "gy", None),
        P(("gx", "gy"), None, None),
        P(("gx", "gy"), None, "gz"),
    )
    return jax.shard_map(body, mesh=mesh, in_specs=in_specs, out_specs=out_specs, check_vma=False)
```

time: 124 us -> 98.7 us (0.80)
  Pallas kernels: 118 us -> 94.9 us
  local copies, waits for them, and re-layouts: 4.47 us -> 2.97 us
    pallas_call x1, Pallas kernels: 118 us -> 93.2 us  [body(): pl.pallas_call(level_kernel, out_shape=(jax.ShapeDtypeStruct((512, 128),...]
    pallas_call x0 -> x1, Pallas kernels: none -> 1.68 us  [body(): pl.pallas_call(deliver_kernel, out_shape=(jax.ShapeDtypeStruct(out.shape,...]
    transpose x2 -> x1, local copies, waits for them, and re-layouts: 2.9 us -> 1.36 us  [body(): return (out.reshape(volume.shape), jnp.transpose(gc[:TAPS], (1, 0, 2)), gb)]
where the time goes in v2:
time: 98.7 us; the launch traced here: 98.5 us
  Pallas kernels  94.9 us (96%)
  local copies, waits for them, and re-layouts  2.97 us (3%)
    pallas_call x1, Pallas kernels, body(): pl.pallas_call(level_kernel, out_shape=(jax.ShapeDtypeStruct((512, 128),...  93.2 us

profile of v2, /device:TPU:1, one launch (start us, length us, event | category | flops | bytes accessed | tf_op | source)
XLA Modules:
  0.0 98.5 jit_solution(14087561930525967262)
XLA Ops:
  0.6 93.2 %level.1 = (bf16[512,128]{1,0:T(8,128)(2,1)}, f32[8,27,128]{2,1,0:T(8,128)}, f32[32,2,128]{2,1,0:T(2,128)}) custom-call(bf16[512,128]{1,0:T(8,128)(2,1)} %bitcast.9, bf16[512,128]{1,0:T(8,128)(2,1)} %bitcast.10, bf16[27,128,128]{2,1,0:T(8,128)(2,1)} %bitcast.8, bf16[8,128,512]{2,1,0:T(8,128)(2,1)} %wd_hbm.1, bf16[27,512,128]{2,1,0:T(8,128)(2,1)} %bitcast.7, ...), custom_call_target="tpu_custom_call" | custom-call | tf_op jit(solution)/shard_map/level/pallas_call | solution.py:643
  93.9 1.7 %deliver.1 = (bf16[512,128]{1,0:T(8,128)(2,1)}, f32[8,27,128]{2,1,0:T(8,128)}) custom-call(bf16[512,128]{1,0:T(8,128)(2,1)} %get-tuple-element.8.out_ref, f32[8,27,128]{2,1,0:T(8,128)} %get-tuple-element.9.gb_ref), custom_call_target="tpu_custom_call" | custom-call | tf_op jit(solution)/shard_map/deliver/pallas_call | solution.py:665
  95.6 1.4 %slice_bitcast_fusion = f32[2,27,128]{2,0,1:T(2,128)} fusion(f32[32,2,128]{2,1,0:T(2,128)} %get-tuple-element.11), kind=kLoop, calls=%fused_computation | loop fusion | bytes 55296 | tf_op jit(solution)/shard_map/transpose | solution.py:672
  96.9 1.6 %copy.9 = f32[8,27,128]{2,0,1:T(8,128)} copy(f32[8,27,128]{2,1,0:T(8,128)} %get-tuple-element.15) | data formatting | bytes 221184

commit v3 on v2

--- a/solution.py
+++ b/solution.py
@@ -63,7 +63,7 @@
     back_out, back_in, bricks, rims, shifted, rim_out, rim_in, corner_out, corner_in, pre_low,
     grad_now, grad_shift, gface_y, gtake_y, gface_x, gtake_x,
     bottle_out, bottle_in, part_acc, part_out, part_in, fine_grad,
-    gb_all, gb_one, gb_ya, gb_xb, gb_a, gb_b, gb_xa, gb_yb, gb_d4, gb_four, gb_d5, gb_five, gb_rows,
+    gb_all, gb_one, gb_ya, gb_ya2, gb_xb, gb_xb2, gb_a, gb_b, gb_xa, gb_xa2, gb_yb, gb_yb2, gb_d4, gb_four, gb_d5, gb_five,
     gc_all, gc_one, gc_xa, gc_yb, gc_a, gc_b, gc_ya, gc_xb, gc_e2, gc_z, gc_half, gc_g,
     send_sem, recv_sem,
 ):
@@ -106,7 +106,7 @@
             shifted[a, side] = jnp.zeros((6, 16, 512), BF)
             grad_shift[a, side] = jnp.zeros((6, 16, 128), BF)
     for tap in range(TAPS, 32):
-        gc_all[tap] = jnp.zeros((4, 32, 128), BF)
+        turned[tap] = jnp.zeros((128, 512), BF)
     gb_all[27] = jnp.zeros((4, 2, 4, 16, 128), BF)
     corner_in[2:4] = jnp.zeros((2, 32, 512), BF)
     for side in range(2):
@@ -251,7 +251,7 @@
     loads[3].wait()
     pre[...] = jnp.zeros_like(pre)
 
-    @pl.loop(0, 9)
+    @pl.loop(0, 9, unroll=3)
     def _(step):
         b, c = step // 3, step % 3
         windows = [
@@ -324,7 +324,7 @@
     pre_low[...] = jnp.zeros_like(pre_low)
 
     def low_taps(first, last):
-        @pl.loop(first, last)
+        @pl.loop(first, last, unroll=3)
         def _(step):
             b, c = step // 3, step % 3
             total = pre_low[...]
@@ -410,7 +410,7 @@
 
     part_acc[...] = jnp.zeros_like(part_acc)
 
-    @pl.loop(0, 9)
+    @pl.loop(0, 9, unroll=3)
     def _(step):
         b, c = step // 3, step % 3
         windows = [grad_shift[2 - a, pl.ds(2 - b, 4), pl.ds(2 - c, 4)].reshape(256, 128) for a in range(3)]
@@ -476,8 +476,51 @@
             copies.append(copy)
         return copies
 
-    gb_second = along_y(lambda y: gb_all.at[pl.ds(mine, 7), y], gb_ya)
-    gb_second += along_x(lambda x: gb_all.at[pl.ds(mine + 7, 7), :, :, x], gb_xb)
+    def y_place(y):
+        return {"gx": 2 * y + zh}
+
+    def x_place(x):
+        return {"gy": 2 * x + core}
+
+    def begin_halving(position, place, mirrored, chunk, inbox):
+        near, far = position ^ 1, 3 - position
+        first, second = (far, near) if mirrored else (near, far)
+        beyond = first ^ 1 if mirrored else 3 - first
+        copies = [
+            remote(chunk(first), inbox.at[0], place(first)), remote(chunk(beyond), inbox.at[1], place(first))
+        ]
+        for copy in copies:
+            copy.start()
+
+        def next_step():
+            copies[1].wait()
+            ref = chunk(second)
+            ref[...] = (ref[...].astype(F32) + inbox[1].astype(F32)).astype(BF)
+            last = remote(ref, inbox.at[2], place(second))
+            last.start()
+            copies[0].wait()
+
+            def finish():
+                own = chunk(position)
+                total = own[...].astype(F32) + inbox[0].astype(F32)
+                last.wait()
+                return total + inbox[2].astype(F32)
+
+            return finish
+
+        return next_step
+
+    parts = ((0, 4), (4, 3))
+    inbox_a, inbox_b = (gb_ya, gb_ya2), (gb_xb, gb_xb2)
+    inbox_c, inbox_d = (gb_xa, gb_xa2), (gb_yb, gb_yb2)
+    gb_steps = []
+    for i, (t, n) in enumerate(parts):
+        gb_steps.append(begin_halving(
+            py, y_place, i == 1, lambda y, t=t, n=n: gb_all.at[pl.ds(mine + t, n), y], inbox_a[i]
+        ))
+        gb_steps.append(begin_halving(
+            px, x_place, i == 1, lambda x, t=t, n=n: gb_all.at[pl.ds(mine + 7 + t, n), :, :, x], inbox_b[i]
+        ))
 
     for copy in part_copies:
         copy.wait()
@@ -491,17 +534,19 @@
         fine_grad[rows] = (spread * slope_sub[rows]).astype(BF)
     fine_grad[...] = matmul(perm_back[...], fine_grad[...]).astype(BF)
 
-    def fine_taps(first, last, base):
-        @pl.loop(first, last)
-        def _(step):
-            term = matmul(turned[base + step], fine_grad[...])
-            gc_all[base + step] = term.astype(BF).reshape(4, 32, 128)
+    def fine_taps(base):
+        for step in range(4):
+            lines = turned[pl.ds(base + 4 * step, 4)].reshape(512, 512)
+            term = matmul(lines, fine_grad[...])
+            gc_all[pl.ds(base + 4 * step, 4)] = term.astype(BF).reshape(4, 4, 32, 128)
 
     keep, give = core * 16, (1 - core) * 16
-    fine_taps(0, 16 - 5 * (1 - core), give)
+    fine_taps(give)
     gc_first = remote(gc_all.at[pl.ds(give, 16)], gc_one, {"gy": gy ^ 1})
     gc_first.start()
-    fine_taps(0, 16 - 5 * core, keep)
+    fine_taps(keep)
+
+    gb_ends = [step() for step in gb_steps]
 
     gc_first.wait()
 
@@ -519,21 +564,16 @@
             total = total + taken[d].astype(F32)
         return total
 
-    for copy in gb_second:
-        copy.wait()
-
-    @pl.loop(0, 7)
-    def _(step):
-        total = gb_all[mine + step, py].astype(F32)
-        other_half = gb_all[mine + 7 + step, :, :, px].astype(F32)
-        for d in range(3):
-            total = total + gb_ya[d, step].astype(F32)
-            other_half = other_half + gb_xb[d, step].astype(F32)
-        gb_a[step] = total.astype(BF)
-        gb_b[step] = other_half.astype(BF)
-
-    gb_third = along_x(lambda x: gb_a.at[:, :, x], gb_xa)
-    gb_third += along_y(lambda y: gb_b.at[:, y], gb_yb)
+    gb_steps = []
+    for i, (t, n) in enumerate(parts):
+        gb_a[t : t + n] = gb_ends[2 * i]().astype(BF)
+        gb_steps.append(begin_halving(
+            px, x_place, i == 1, lambda x, t=t, n=n: gb_a.at[pl.ds(t, n), :, x], inbox_c[i]
+        ))
+        gb_b[t : t + n] = gb_ends[2 * i + 1]().astype(BF)
+        gb_steps.append(begin_halving(
+            py, y_place, i == 1, lambda y, t=t, n=n: gb_b.at[pl.ds(t, n), y], inbox_d[i]
+        ))
 
     for copy in gc_second:
         copy.wait()
@@ -542,10 +582,10 @@
     gc_third = along_y(lambda y: gc_a.at[:, y], gc_ya)
     gc_third += along_x(lambda x: gc_b.at[pl.ds(2 * x, 2)], gc_xb)
 
-    for copy in gb_third:
-        copy.wait()
-    gb_d4[0:7] = summed(gb_a[:, :, px], gb_xa).astype(BF)
-    gb_d4[7:14] = summed(gb_b[:, py], gb_yb).astype(BF)
+    gb_last = [step() for step in gb_steps]
+    for i, (t, n) in enumerate(parts):
+        gb_d4[t : t + n] = gb_last[2 * i]().astype(BF)
+        gb_d4[7 + t : 7 + t + n] = gb_last[2 * i + 1]().astype(BF)
     gb_fourth = remote(gb_d4.at[:, 1 - zh], gb_four, {"gx": gx ^ 1})
     gb_fourth.start()
 
@@ -587,10 +627,8 @@
     gc_g[gy] = gc_half[gy >> 2]
 
     gb_fifth.wait()
-    for step in range(14):
-        gb_rows[pl.ds(mine + step, 8, stride=32), :] = gb_d5[step, core]
-        gb_rows[pl.ds(other + step, 8, stride=32), :] = gb_five[step]
-    gb_ref[...] = gb_rows[...].reshape(8, 32, 128)[:, 0:TAPS]
+    gb_ref[pl.ds(mine, 14)] = gb_d5[:, core]
+    gb_ref[pl.ds(other, 14)] = gb_five[...]
 
     for copy in gathers:
         copy.wait()
@@ -605,9 +643,10 @@
         gc_ref[first + 8 : first + 10] = chosen[2:4]
 
 
-def deliver_kernel(out_ref, gb_ref, out_final, gb_final):
+def deliver_kernel(out_ref, gb_ref, gc_ref, out_final, gb_final, gc_final):
     out_final[...] = out_ref[...]
-    gb_final[...] = gb_ref[...]
+    gb_final[...] = gb_ref[0:TAPS]
+    gc_final[...] = gc_ref[0:TAPS]
 
 
 def body(volume, cotangent, w_conv, w_down, w_bottle, w_up):
@@ -623,7 +662,7 @@
         kept(512, 512), kept(512, 512), kept(512, 512), kept(512, 512), kept(512, 512),
         kept(3, 256, 256), kept(3, 128, 128), kept(256, 256), kept(3, 128, 128),
         kept(2, 64, 128), kept(2, 80, 128), kept(2, 80, 128), kept(2, 112, 128), kept(2, 112, 128),
-        vmem((10, 10, 24, 128), F32), kept(27, 512, 128), kept(27, 128, 512), vmem((512, 128), F32),
+        vmem((10, 10, 24, 128), F32), kept(27, 512, 128), kept(32, 128, 512), vmem((512, 128), F32),
         kept(512, 128), vmem((512, 128), F32), kept(512, 128),
         kept(4, 64, 128), kept(4, 64, 128), kept(4, 64, 512), kept(4, 32, 512), kept(3, 6, 6, 16, 512),
         kept(2, 64, 512), kept(2, 64, 512), kept(2, 32, 512), kept(4, 32, 512), vmem((256, 128), F32),
@@ -631,10 +670,11 @@
         kept(2, 96, 128), kept(2, 128, 128),
         kept(4, 64, 128), kept(4, 64, 128), vmem((256, 512), F32), kept(4, 64, 512),
         kept(3, 64, 512), kept(512, 128),
-        kept(28, 4, 2, 4, 16, 128), kept(14, 4, 2, 4, 16, 128), kept(3, 7, 2, 4, 16, 128), kept(3, 7, 4, 2, 16, 128),
-        kept(7, 2, 4, 16, 128), kept(7, 4, 2, 16, 128), kept(3, 7, 2, 16, 128), kept(3, 7, 2, 16, 128),
+        kept(28, 4, 2, 4, 16, 128), kept(14, 4, 2, 4, 16, 128),
+        kept(3, 4, 2, 4, 16, 128), kept(3, 3, 2, 4, 16, 128), kept(3, 4, 4, 2, 16, 128), kept(3, 3, 4, 2, 16, 128),
+        kept(7, 2, 4, 16, 128), kept(7, 4, 2, 16, 128),
+        kept(3, 4, 2, 16, 128), kept(3, 3, 2, 16, 128), kept(3, 4, 2, 16, 128), kept(3, 3, 2, 16, 128),
         kept(14, 2, 16, 128), kept(14, 16, 128), vmem((14, 2, 8, 128), F32), vmem((14, 8, 128), F32),
-        vmem((256, 128), F32),
         kept(32, 4, 32, 128), kept(16, 4, 32, 128), kept(3, 2, 4, 32, 128), kept(3, 8, 32, 128),
         kept(2, 4, 32, 128), kept(8, 32, 128), kept(3, 2, 32, 128), kept(3, 2, 32, 128),
         kept(4, 2, 16, 128), kept(8, 4, 16, 128), vmem((2, 4, 8, 128), F32), vmem((8, 4, 8, 128), F32),
@@ -644,7 +684,7 @@
         level_kernel,
         out_shape=(
             jax.ShapeDtypeStruct((512, 128), BF),
-            jax.ShapeDtypeStruct((8, TAPS, 128), F32),
+            jax.ShapeDtypeStruct((28, 8, 128), F32),
             jax.ShapeDtypeStruct((32, 2, 128), F32),
         ),
         in_specs=[whole] * 6,
@@ -662,14 +702,18 @@
         jnp.transpose(w_bottle, (1, 0, 2)),
         w_up,
     )
-    out, gb = pl.pallas_call(
+    out, gb, gc = pl.pallas_call(
         deliver_kernel,
-        out_shape=(jax.ShapeDtypeStruct(out.shape, BF), jax.ShapeDtypeStruct(gb.shape, F32)),
-        in_specs=[held] * 2,
-        out_specs=(held,) * 2,
+        out_shape=(
+            jax.ShapeDtypeStruct(out.shape, BF),
+            jax.ShapeDtypeStruct((TAPS, 8, 128), F32),
+            jax.ShapeDtypeStruct((TAPS, 2, 128), F32),
+        ),
+        in_specs=[held] * 3,
+        out_specs=(held,) * 3,
         name="deliver",
-    )(out, gb)
-    return out.reshape(volume.shape), jnp.transpose(gc[:TAPS], (1, 0, 2)), gb
+    )(out, gb, gc)
+    return out.reshape(volume.shape), jnp.transpose(gc, (1, 0, 2)), jnp.transpose(gb, (1, 0, 2))
 
 
 def solution(mesh):

time: 98.7 us -> 95.8 us (0.971)
  local copies, waits for them, and re-layouts: 2.97 us -> 0 us
    unnamed x1 -> x0, local copies, waits for them, and re-layouts: 1.62 us -> none
    transpose x1 -> x0, local copies, waits for them, and re-layouts: 1.36 us -> none  [body(): return (out.reshape(volume.shape), jnp.transpose(gc[:TAPS], (1, 0, 2)), gb)]
where the time goes in v3:
time: 95.8 us; the launch traced here: 95.7 us
  Pallas kernels  95.1 us (99%)
    pallas_call x1, Pallas kernels, body(): pl.pallas_call(level_kernel, out_shape=(jax.ShapeDtypeStruct((512, 128),...  93.4 us

profile of v3, /device:TPU:1, one launch (start us, length us, event | category | flops | bytes accessed | tf_op | source)
XLA Modules:
  0.0 95.7 jit_solution(15709801858471796671)
XLA Ops:
  0.6 93.4 %level.1 = (bf16[512,128]{1,0:T(8,128)(2,1)}, f32[28,8,128]{2,1,0:T(8,128)}, f32[32,2,128]{2,1,0:T(2,128)}) custom-call(bf16[512,128]{1,0:T(8,128)(2,1)} %bitcast.9, bf16[512,128]{1,0:T(8,128)(2,1)} %bitcast.10, bf16[27,128,128]{2,1,0:T(8,128)(2,1)} %bitcast.8, bf16[8,128,512]{2,1,0:T(8,128)(2,1)} %wd_hbm.1, bf16[27,512,128]{2,1,0:T(8,128)(2,1)} %bitcast.7, ...), custom_call_target="tpu_custom_call" | custom-call | tf_op jit(solution)/shard_map/level/pallas_call | solution.py:683
  94.0 1.7 %deliver.1 = (bf16[512,128]{1,0:T(8,128)(2,1)}, f32[27,8,128]{2,1,0:T(8,128)}, f32[27,2,128]{2,1,0:T(2,128)}) custom-call(bf16[512,128]{1,0:T(8,128)(2,1)} %get-tuple-element.9.out_ref, f32[28,8,128]{2,1,0:T(8,128)} %get-tuple-element.10.gb_ref, f32[32,2,128]{2,1,0:T(2,128)} %get-tuple-element.11.gc_ref), custom_call_target="tpu_custom_call" | custom-call | tf_op jit(solution)/shard_map/deliver/pallas_call | solution.py:705

commit v4 on v3

--- a/solution.py
+++ b/solution.py
@@ -546,8 +546,6 @@
     gc_first.start()
     fine_taps(keep)
 
-    gb_ends = [step() for step in gb_steps]
-
     gc_first.wait()
 
     @pl.loop(0, 16)
@@ -557,12 +555,21 @@
 
     gc_second = along_x(lambda x: gc_all.at[pl.ds(keep + 2 * x, 2)], gc_xa)
     gc_second += along_y(lambda y: gc_all.at[pl.ds(keep + 8, 8), y], gc_yb)
+
+    gb_ends = [step() for step in gb_steps]
 
     def summed(own, taken):
         total = own.astype(F32)
         for d in range(3):
             total = total + taken[d].astype(F32)
         return total
+
+    for copy in gc_second:
+        copy.wait()
+    gc_a[...] = summed(gc_all[pl.ds(keep + 2 * px, 2)], gc_xa).astype(BF)
+    gc_b[...] = summed(gc_all[pl.ds(keep + 8, 8), py], gc_yb).astype(BF)
+    gc_third = along_y(lambda y: gc_a.at[:, y], gc_ya)
+    gc_third += along_x(lambda x: gc_b.at[pl.ds(2 * x, 2)], gc_xb)
 
     gb_steps = []
     for i, (t, n) in enumerate(parts):
@@ -574,20 +581,6 @@
         gb_steps.append(begin_halving(
             py, y_place, i == 1, lambda y, t=t, n=n: gb_b.at[pl.ds(t, n), y], inbox_d[i]
         ))
-
-    for copy in gc_second:
-        copy.wait()
-    gc_a[...] = summed(gc_all[pl.ds(keep + 2 * px, 2)], gc_xa).astype(BF)
-    gc_b[...] = summed(gc_all[pl.ds(keep + 8, 8), py], gc_yb).astype(BF)
-    gc_third = along_y(lambda y: gc_a.at[:, y], gc_ya)
-    gc_third += along_x(lambda x: gc_b.at[pl.ds(2 * x, 2)], gc_xb)
-
-    gb_last = [step() for step in gb_steps]
-    for i, (t, n) in enumerate(parts):
-        gb_d4[t : t + n] = gb_last[2 * i]().astype(BF)
-        gb_d4[7 + t : 7 + t + n] = gb_last[2 * i + 1]().astype(BF)
-    gb_fourth = remote(gb_d4.at[:, 1 - zh], gb_four, {"gx": gx ^ 1})
-    gb_fourth.start()
 
     for copy in gc_third:
         copy.wait()
@@ -606,10 +599,12 @@
             gc_fourth.append(copy)
     gc_z[slot] = gc_e2[:, zh]
 
-    gb_fourth.wait()
-    gb_d5[...] = (gb_d4[:, zh].astype(F32) + gb_four[...].astype(F32)).reshape(14, 2, 8, 128)
-    gb_fifth = remote(gb_d5.at[:, 1 - core], gb_five, {"gy": gy ^ 1})
-    gb_fifth.start()
+    gb_last = [step() for step in gb_steps]
+    for i, (t, n) in enumerate(parts):
+        gb_d4[t : t + n] = gb_last[2 * i]().astype(BF)
+        gb_d4[7 + t : 7 + t + n] = gb_last[2 * i + 1]().astype(BF)
+    gb_fourth = remote(gb_d4.at[:, 1 - zh], gb_four, {"gx": gx ^ 1})
+    gb_fourth.start()
 
     for copy in gc_fourth:
         copy.wait()
@@ -625,6 +620,11 @@
         copy.start()
         gathers.append(copy)
     gc_g[gy] = gc_half[gy >> 2]
+
+    gb_fourth.wait()
+    gb_d5[...] = (gb_d4[:, zh].astype(F32) + gb_four[...].astype(F32)).reshape(14, 2, 8, 128)
+    gb_fifth = remote(gb_d5.at[:, 1 - core], gb_five, {"gy": gy ^ 1})
+    gb_fifth.start()
 
     gb_fifth.wait()
     gb_ref[pl.ds(mine, 14)] = gb_d5[:, core]

time: 95.8 us -> 89.1 us (0.930)
  Pallas kernels: 95.1 us -> 87.6 us
    pallas_call x1, Pallas kernels: 93.4 us -> 85.9 us  [body(): pl.pallas_call(level_kernel, out_shape=(jax.ShapeDtypeStruct((512, 128),...]
where the time goes in v4:
time: 89.1 us; the launch traced here: 88.3 us
  Pallas kernels  87.6 us (98%)
    pallas_call x1, Pallas kernels, body(): pl.pallas_call(level_kernel, out_shape=(jax.ShapeDtypeStruct((512, 128),...  85.9 us

profile of v4, /device:TPU:1, one launch (start us, length us, event | category | flops | bytes accessed | tf_op | source)
XLA Modules:
  0.0 88.3 jit_solution(11602383915005596911)
XLA Ops:
  0.6 85.9 %level.1 = (bf16[512,128]{1,0:T(8,128)(2,1)}, f32[28,8,128]{2,1,0:T(8,128)}, f32[32,2,128]{2,1,0:T(2,128)}) custom-call(bf16[512,128]{1,0:T(8,128)(2,1)} %bitcast.9, bf16[512,128]{1,0:T(8,128)(2,1)} %bitcast.10, bf16[27,128,128]{2,1,0:T(8,128)(2,1)} %bitcast.8, bf16[8,128,512]{2,1,0:T(8,128)(2,1)} %wd_hbm.1, bf16[27,512,128]{2,1,0:T(8,128)(2,1)} %bitcast.7, ...), custom_call_target="tpu_custom_call" | custom-call | tf_op jit(solution)/shard_map/level/pallas_call | solution.py:683
  86.6 1.7 %deliver.1 = (bf16[512,128]{1,0:T(8,128)(2,1)}, f32[27,8,128]{2,1,0:T(8,128)}, f32[27,2,128]{2,1,0:T(2,128)}) custom-call(bf16[512,128]{1,0:T(8,128)(2,1)} %get-tuple-element.9.out_ref, f32[28,8,128]{2,1,0:T(8,128)} %get-tuple-element.10.gb_ref, f32[32,2,128]{2,1,0:T(2,128)} %get-tuple-element.11.gc_ref), custom_call_target="tpu_custom_call" | custom-call | tf_op jit(solution)/shard_map/deliver/pallas_call | solution.py:705

commit v5 on v4

--- a/solution.py
+++ b/solution.py
@@ -9,7 +9,7 @@
 F32 = jnp.float32
 MESH = pl.DeviceIdType.MESH
 TAPS = 27
-COPIES = 96
+COPIES = 112
 
 
 def matmul(left, right):
@@ -58,7 +58,7 @@
     out_ref, gb_ref, gc_ref,
     vol, cot, wc, wd, wb, wu, load_sem,
     perm_xyz, perm_sub, perm_cot, perm_back, perm_out, perm_group, perm_rim, perm_brick, lift_z,
-    plane_z, face_y, take_y, face_x, take_x,
+    plane_z, face_main, take_main, face_y, take_y, face_x, take_x,
     padded, columns, turned, pre, cot_sub, slope_sub, hidden_sub,
     back_out, back_in, bricks, rims, shifted, rim_out, rim_in, corner_out, corner_in, pre_low,
     grad_now, grad_shift, gface_y, gtake_y, gface_x, gtake_x,
@@ -167,6 +167,14 @@
 
     finish_z = exchange(
         "gz", gz, 4, vol.at[pl.ds(0, 64)], plane_z.at[1], vol.at[pl.ds(448, 64)], plane_z.at[0]
+    )
+
+    main = matmul(perm_xyz[...], vol[...])
+    padded[1:9, 1:9, 8:16, :] = main.reshape(8, 8, 8, 128)
+    face_main[0] = main[0:64].astype(BF)
+    face_main[1] = main[448:512].astype(BF)
+    finish_main = exchange(
+        "gx", gx, 8, face_main.at[0], take_main.at[1], face_main.at[1], take_main.at[0]
     )
 
     loads[1].wait()
@@ -185,8 +193,6 @@
         back_copies.append(copy)
     back_in[gz] = back_out[gz]
 
-    main = matmul(perm_xyz[...], vol[...])
-    padded[1:9, 1:9, 8:16, :] = main.reshape(8, 8, 8, 128)
     flat = padded.reshape(2400, 128)
 
     def at_row(x, y, z):
@@ -232,21 +238,13 @@
     finish_y(lambda: put_y(0, 0), lambda: put_y(1, 9))
 
     for side, x in ((0, 1), (1, 8)):
-        face_x[side, 0:80] = padded[x, 0:10, 8:16, :].reshape(80, 128).astype(BF)
+        ends = [padded[x, y, 8:16, :] for y in (0, 9)]
+        face_x[side, 0:16] = jnp.concatenate(ends, axis=0).astype(BF)
         for i, z in enumerate((0, 9)):
             first = flat[pl.ds(at_row(x, 0, z), 8, stride=24), :]
             rest = flat[pl.ds(at_row(x, 2, z), 8, stride=24), :]
-            face_x[side, 80 + 16 * i : 96 + 16 * i] = jnp.concatenate([first, rest], axis=0).astype(BF)
+            face_x[side, 16 + 16 * i : 32 + 16 * i] = jnp.concatenate([first, rest], axis=0).astype(BF)
     finish_x = exchange("gx", gx, 8, face_x.at[0], take_x.at[1], face_x.at[1], take_x.at[0])
-
-    def put_x(side, x):
-        face = take_x[side].astype(F32)
-        padded[x, 0:10, 8:16, :] = face[0:80].reshape(10, 8, 128)
-        for i, z in enumerate((0, 9)):
-            flat[pl.ds(at_row(x, 0, z), 8, stride=24), :] = face[80 + 16 * i : 88 + 16 * i]
-            flat[pl.ds(at_row(x, 2, z), 8, stride=24), :] = face[88 + 16 * i : 96 + 16 * i]
-
-    finish_x(lambda: put_x(0, 0), lambda: put_x(1, 9))
 
     loads[3].wait()
     pre[...] = jnp.zeros_like(pre)
@@ -261,6 +259,28 @@
             columns[a * 9 + step] = windows[a]
         weights = jnp.concatenate([wc[a * 9 + step] for a in range(3)], axis=0)
         pre[...] += matmul(jnp.concatenate(windows, axis=1), weights)
+
+    def put_main(side, x):
+        padded[x, 1:9, 8:16, :] = take_main[side].astype(F32).reshape(8, 8, 128)
+
+    def put_x(side, x):
+        face = take_x[side].astype(F32)
+        padded[x, 0, 8:16, :] = face[0:8]
+        padded[x, 9, 8:16, :] = face[8:16]
+        for i, z in enumerate((0, 9)):
+            flat[pl.ds(at_row(x, 0, z), 8, stride=24), :] = face[16 + 16 * i : 24 + 16 * i]
+            flat[pl.ds(at_row(x, 2, z), 8, stride=24), :] = face[24 + 16 * i : 32 + 16 * i]
+
+    finish_main(lambda: put_main(0, 0), lambda: put_main(1, 9))
+    finish_x(lambda: put_x(0, 0), lambda: put_x(1, 9))
+
+    for c in range(3):
+        for x, first, b in ((0, 0, 0), (9, 448, 2)):
+            windows = [padded[x, c : c + 8, 7 + a : 15 + a, :].reshape(64, 128).astype(BF) for a in range(3)]
+            for a in range(3):
+                columns[a * 9 + 3 * b + c, first : first + 64] = windows[a]
+            weights = jnp.concatenate([wc[a * 9 + 3 * b + c] for a in range(3)], axis=0)
+            pre[first : first + 64] += matmul(jnp.concatenate(windows, axis=1), weights)
 
     high = pre[...].astype(BF)
     low = (pre[...] - high.astype(F32)).astype(BF)
@@ -661,7 +681,8 @@
         kept(27, 512, 128), kept(8, 512, 128), pltpu.SemaphoreType.DMA((6,)),
         kept(512, 512), kept(512, 512), kept(512, 512), kept(512, 512), kept(512, 512),
         kept(3, 256, 256), kept(3, 128, 128), kept(256, 256), kept(3, 128, 128),
-        kept(2, 64, 128), kept(2, 80, 128), kept(2, 80, 128), kept(2, 112, 128), kept(2, 112, 128),
+        kept(2, 64, 128), kept(2, 64, 128), kept(2, 64, 128), kept(2, 80, 128), kept(2, 80, 128),
+        kept(2, 48, 128), kept(2, 48, 128),
         vmem((10, 10, 24, 128), F32), kept(27, 512, 128), kept(32, 128, 512), vmem((512, 128), F32),
         kept(512, 128), vmem((512, 128), F32), kept(512, 128),
         kept(4, 64, 128), kept(4, 64, 128), kept(4, 64, 512), kept(4, 32, 512), kept(3, 6, 6, 16, 512),

time: 89.1 us -> 87.6 us (0.983)
  no operation moved by 1% of the time
where the time goes in v5:
time: 87.6 us; the launch traced here: 87.5 us
  Pallas kernels  86.9 us (99%)
    pallas_call x1, Pallas kernels, body(): pl.pallas_call(level_kernel, out_shape=(jax.ShapeDtypeStruct((512, 128),...  85.2 us

profile of v5, /device:TPU:1, one launch (start us, length us, event | category | flops | bytes accessed | tf_op | source)
XLA Modules:
  0.0 87.5 jit_solution(10758355284496606545)
XLA Ops:
  0.6 85.2 %level.1 = (bf16[512,128]{1,0:T(8,128)(2,1)}, f32[28,8,128]{2,1,0:T(8,128)}, f32[32,2,128]{2,1,0:T(2,128)}) custom-call(bf16[512,128]{1,0:T(8,128)(2,1)} %bitcast.9, bf16[512,128]{1,0:T(8,128)(2,1)} %bitcast.10, bf16[27,128,128]{2,1,0:T(8,128)(2,1)} %bitcast.8, bf16[8,128,512]{2,1,0:T(8,128)(2,1)} %wd_hbm.1, bf16[27,512,128]{2,1,0:T(8,128)(2,1)} %bitcast.7, ...), custom_call_target="tpu_custom_call" | custom-call | tf_op jit(solution)/shard_map/level/pallas_call | solution.py:704
  85.9 1.7 %deliver.1 = (bf16[512,128]{1,0:T(8,128)(2,1)}, f32[27,8,128]{2,1,0:T(8,128)}, f32[27,2,128]{2,1,0:T(2,128)}) custom-call(bf16[512,128]{1,0:T(8,128)(2,1)} %get-tuple-element.9.out_ref, f32[28,8,128]{2,1,0:T(8,128)} %get-tuple-element.10.gb_ref, f32[32,2,128]{2,1,0:T(2,128)} %get-tuple-element.11.gc_ref), custom_call_target="tpu_custom_call" | custom-call | tf_op jit(solution)/shard_map/deliver/pallas_call | solution.py:726

commit v6 on v5

--- a/solution.py
+++ b/solution.py
@@ -57,7 +57,7 @@
     vol_hbm, cot_hbm, wc_hbm, wd_hbm, wb_hbm, wu_hbm,
     out_ref, gb_ref, gc_ref,
     vol, cot, wc, wd, wb, wu, load_sem,
-    perm_xyz, perm_sub, perm_cot, perm_back, perm_out, perm_group, perm_rim, perm_brick, lift_z,
+    perm_xyz, perm_sub, perm_cot, perm_back, perm_out, perm_group, perm_rim, perm_brick, perm_part, lift_z,
     plane_z, face_main, take_main, face_y, take_y, face_x, take_x,
     padded, columns, turned, pre, cot_sub, slope_sub, hidden_sub,
     back_out, back_in, bricks, rims, shifted, rim_out, rim_in, corner_out, corner_in, pre_low,
@@ -100,6 +100,57 @@
     for load in loads:
         load.start()
 
+    def sub_to_xyz(row):
+        x, y, z = cell_of_sub(row)
+        return (x * 8 + y) * 8 + z
+
+    def sub_to_zxy(row):
+        x, y, z = cell_of_sub(row)
+        return (z * 8 + x) * 8 + y
+
+    perm_xyz[...] = selection(512, 512, lambda r: ((r & 7) * 8 + (r >> 6)) * 8 + ((r >> 3) & 7))
+
+    loads[0].wait()
+    main = matmul(perm_xyz[...], vol[...])
+    face_main[0] = main[0:64].astype(BF)
+    face_main[1] = main[448:512].astype(BF)
+    pl.semaphore_wait(barrier, len(partners))
+
+    def exchange(axis, position, count, low_src, high_dst, high_src, low_dst):
+        down = remote(low_src, high_dst, {axis: around(position, count - 1, count)})
+        up = remote(high_src, low_dst, {axis: around(position, 1, count)})
+
+        @pl.when(position > 0)
+        def _():
+            down.start()
+
+        @pl.when(position < count - 1)
+        def _():
+            up.start()
+
+        def finish(on_low, on_high):
+            @pl.when(position > 0)
+            def _():
+                down.wait_send()
+                up.wait_recv()
+                on_low()
+
+            @pl.when(position < count - 1)
+            def _():
+                up.wait_send()
+                down.wait_recv()
+                on_high()
+
+        return finish
+
+    finish_z = exchange(
+        "gz", gz, 4, vol.at[pl.ds(0, 64)], plane_z.at[1], vol.at[pl.ds(448, 64)], plane_z.at[0]
+    )
+
+    finish_main = exchange(
+        "gx", gx, 8, face_main.at[0], take_main.at[1], face_main.at[1], take_main.at[0]
+    )
+
     padded[...] = jnp.zeros_like(padded)
     for side in (0, 5):
         for a in range(3):
@@ -123,59 +174,8 @@
             rim_in[side] = jnp.zeros((64, 512), BF)
             corner_in[side] = jnp.zeros((32, 512), BF)
             gtake_y[side] = jnp.zeros((64, 128), BF)
-
-    def sub_to_xyz(row):
-        x, y, z = cell_of_sub(row)
-        return (x * 8 + y) * 8 + z
-
-    def sub_to_zxy(row):
-        x, y, z = cell_of_sub(row)
-        return (z * 8 + x) * 8 + y
-
-    perm_xyz[...] = selection(512, 512, lambda r: ((r & 7) * 8 + (r >> 6)) * 8 + ((r >> 3) & 7))
+    padded[1:9, 1:9, 8:16, :] = main.reshape(8, 8, 8, 128)
     perm_cot[...] = selection(512, 512, sub_to_zxy)
-
-    loads[0].wait()
-    pl.semaphore_wait(barrier, len(partners))
-
-    def exchange(axis, position, count, low_src, high_dst, high_src, low_dst):
-        down = remote(low_src, high_dst, {axis: around(position, count - 1, count)})
-        up = remote(high_src, low_dst, {axis: around(position, 1, count)})
-
-        @pl.when(position > 0)
-        def _():
-            down.start()
-
-        @pl.when(position < count - 1)
-        def _():
-            up.start()
-
-        def finish(on_low, on_high):
-            @pl.when(position > 0)
-            def _():
-                down.wait_send()
-                up.wait_recv()
-                on_low()
-
-            @pl.when(position < count - 1)
-            def _():
-                up.wait_send()
-                down.wait_recv()
-                on_high()
-
-        return finish
-
-    finish_z = exchange(
-        "gz", gz, 4, vol.at[pl.ds(0, 64)], plane_z.at[1], vol.at[pl.ds(448, 64)], plane_z.at[0]
-    )
-
-    main = matmul(perm_xyz[...], vol[...])
-    padded[1:9, 1:9, 8:16, :] = main.reshape(8, 8, 8, 128)
-    face_main[0] = main[0:64].astype(BF)
-    face_main[1] = main[448:512].astype(BF)
-    finish_main = exchange(
-        "gx", gx, 8, face_main.at[0], take_main.at[1], face_main.at[1], take_main.at[0]
-    )
 
     loads[1].wait()
     cot_sub[...] = matmul(perm_cot[...], cot[...]).astype(BF)
@@ -214,6 +214,8 @@
     perm_sub[...] = selection(512, 512, sub_to_xyz)
     perm_back[...] = selection(512, 512, lambda r: sub_of_cell(r >> 6, (r >> 3) & 7, r & 7))
     perm_out[...] = selection(512, 512, lambda r: sub_of_cell((r >> 3) & 7, r & 7, r >> 6))
+
+    perm_part[...] = selection(128, 128, lambda r: ((r & 31) >> 2) * 16 + (r >> 5) * 4 + (r & 3))
 
     def shifted_z(r, shift, column_of):
         z = (r & 15) + shift
@@ -437,6 +439,17 @@
         weights = jnp.concatenate([wb[a * 9 + step] for a in range(3)], axis=1)
         part_acc[...] += matmul_nt(jnp.concatenate(windows, axis=1), weights)
 
+    part_copies = []
+
+    def send_parts(which, rows):
+        part_out[which] = matmul(perm_part[...], rows.astype(BF)).astype(BF).reshape(4, 32, 512)
+        for d in (1, 2, 3):
+            peer = around(gz, d, 4)
+            copy = remote(part_out.at[which, peer], part_in.at[which, d - 1], {"gz": peer})
+            copy.start()
+            part_copies.append(copy)
+
+    send_parts(0, part_acc[64:192])
     finish_gx(lambda: None, lambda: None)
     for a in range(3):
         for side, x in ((0, 0), (1, 5)):
@@ -450,28 +463,12 @@
             weights = jnp.concatenate([wb[a * 9 + 3 * b + c] for a in range(3)], axis=1)
             part_acc[rows : rows + 64] += matmul_nt(jnp.concatenate(windows, axis=1), weights)
 
-    part_out[...] = matmul(perm_brick[...], part_acc[...].astype(BF)).astype(BF).reshape(4, 64, 512)
-    part_copies = []
-    for d in (1, 2, 3):
-        peer = around(gz, d, 4)
-        copy = remote(part_out.at[peer], part_in.at[d - 1], {"gz": peer})
-        copy.start()
-        part_copies.append(copy)
+    send_parts(1, jnp.concatenate([part_acc[0:64], part_acc[192:256]], axis=0))
 
     bottle_taps(8, 13 + core, other)
     gb_first = remote(gb_all.at[pl.ds(other, 14)], gb_one, {"gy": gy ^ 1})
     gb_first.start()
     bottle_taps(0, 14 - core, mine)
-
-    for copy in bottle_copies:
-        copy.wait()
-    for s in range(8):
-        lifted = jnp.zeros((64, 128), F32)
-        for q in range(4):
-            lifted = lifted + matmul(bottle_in[q], wu[s, pl.ds(128 * q, 128)])
-        total = lifted + hidden_sub[pl.ds(64 * s, 64)].astype(F32)
-        fine_grad[pl.ds(64 * s, 64)] = total.astype(BF)
-    out_ref[...] = matmul(perm_out[...], fine_grad[...]).astype(BF)
 
     gb_first.wait()
 
@@ -544,10 +541,14 @@
 
     for copy in part_copies:
         copy.wait()
-    coarse_grad = part_out[gz].astype(F32)
-    for d in range(3):
-        coarse_grad = coarse_grad + part_in[d].astype(F32)
-    coarse_grad = coarse_grad.astype(BF)
+    sums = []
+    for which in range(2):
+        total = part_out[which, gz].astype(F32)
+        for d in range(3):
+            total = total + part_in[which, d].astype(F32)
+        sums.append(total)
+    inner, outer = sums
+    coarse_grad = jnp.concatenate([outer[0:16], inner, outer[16:32]], axis=0).astype(BF)
     for s in range(8):
         rows = pl.ds(64 * s, 64)
         spread = matmul_nt(coarse_grad, wd[s]) + cot_sub[rows].astype(F32)
@@ -626,6 +627,16 @@
     gb_fourth = remote(gb_d4.at[:, 1 - zh], gb_four, {"gx": gx ^ 1})
     gb_fourth.start()
 
+    for copy in bottle_copies:
+        copy.wait()
+    for s in range(8):
+        lifted = jnp.zeros((64, 128), F32)
+        for q in range(4):
+            lifted = lifted + matmul(bottle_in[q], wu[s, pl.ds(128 * q, 128)])
+        total = lifted + hidden_sub[pl.ds(64 * s, 64)].astype(F32)
+        fine_grad[pl.ds(64 * s, 64)] = total.astype(BF)
+    out_ref[...] = matmul(perm_out[...], fine_grad[...]).astype(BF)
+
     for copy in gc_fourth:
         copy.wait()
     total = gc_z[0].astype(F32)
@@ -680,7 +691,7 @@
         kept(512, 128), kept(512, 128), kept(27, 128, 128), kept(8, 128, 512),
         kept(27, 512, 128), kept(8, 512, 128), pltpu.SemaphoreType.DMA((6,)),
         kept(512, 512), kept(512, 512), kept(512, 512), kept(512, 512), kept(512, 512),
-        kept(3, 256, 256), kept(3, 128, 128), kept(256, 256), kept(3, 128, 128),
+        kept(3, 256, 256), kept(3, 128, 128), kept(256, 256), kept(128, 128), kept(3, 128, 128),
         kept(2, 64, 128), kept(2, 64, 128), kept(2, 64, 128), kept(2, 80, 128), kept(2, 80, 128),
         kept(2, 48, 128), kept(2, 48, 128),
         vmem((10, 10, 24, 128), F32), kept(27, 512, 128), kept(32, 128, 512), vmem((512, 128), F32),
@@ -689,8 +700,8 @@
         kept(2, 64, 512), kept(2, 64, 512), kept(2, 32, 512), kept(4, 32, 512), vmem((256, 128), F32),
         kept(256, 128), kept(3, 6, 6, 16, 128), kept(2, 64, 128), kept(2, 64, 128),
         kept(2, 96, 128), kept(2, 128, 128),
-        kept(4, 64, 128), kept(4, 64, 128), vmem((256, 512), F32), kept(4, 64, 512),
-        kept(3, 64, 512), kept(512, 128),
+        kept(4, 64, 128), kept(4, 64, 128), vmem((256, 512), F32), kept(2, 4, 32, 512),
+        kept(2, 3, 32, 512), kept(512, 128),
         kept(28, 4, 2, 4, 16, 128), kept(14, 4, 2, 4, 16, 128),
         kept(3, 4, 2, 4, 16, 128), kept(3, 3, 2, 4, 16, 128), kept(3, 4, 4, 2, 16, 128), kept(3, 3, 4, 2, 16, 128),
         kept(7, 2, 4, 16, 128), kept(7, 4, 2, 16, 128),

time: 87.6 us -> 88.5 us (1.010); the launches traced: 87.5 us -> 87.5 us
  no operation moved by 1% of the time
where the time goes in v6:
time: 88.5 us; the launch traced here: 87.5 us
  Pallas kernels  86.8 us (98%)
    pallas_call x1, Pallas kernels, body(): pl.pallas_call(level_kernel, out_shape=(jax.ShapeDtypeStruct((512, 128),...  85.2 us

profile of v6, /device:TPU:1, one launch (start us, length us, event | category | flops | bytes accessed | tf_op | source)
XLA Modules:
  0.0 87.5 jit_solution(12481925154247975735)
XLA Ops:
  0.6 85.2 %level.1 = (bf16[512,128]{1,0:T(8,128)(2,1)}, f32[28,8,128]{2,1,0:T(8,128)}, f32[32,2,128]{2,1,0:T(2,128)}) custom-call(bf16[512,128]{1,0:T(8,128)(2,1)} %bitcast.9, bf16[512,128]{1,0:T(8,128)(2,1)} %bitcast.10, bf16[27,128,128]{2,1,0:T(8,128)(2,1)} %bitcast.8, bf16[8,128,512]{2,1,0:T(8,128)(2,1)} %wd_hbm.1, bf16[27,512,128]{2,1,0:T(8,128)(2,1)} %bitcast.7, ...), custom_call_target="tpu_custom_call" | custom-call | tf_op jit(solution)/shard_map/level/pallas_call | solution.py:715
  85.8 1.7 %deliver.1 = (bf16[512,128]{1,0:T(8,128)(2,1)}, f32[27,8,128]{2,1,0:T(8,128)}, f32[27,2,128]{2,1,0:T(2,128)}) custom-call(bf16[512,128]{1,0:T(8,128)(2,1)} %get-tuple-element.9.out_ref, f32[28,8,128]{2,1,0:T(8,128)} %get-tuple-element.10.gb_ref, f32[32,2,128]{2,1,0:T(2,128)} %get-tuple-element.11.gc_ref), custom_call_target="tpu_custom_call" | custom-call | tf_op jit(solution)/shard_map/deliver/pallas_call | solution.py:737

commit v7 on v6

--- a/solution.py
+++ b/solution.py
@@ -57,7 +57,7 @@
     vol_hbm, cot_hbm, wc_hbm, wd_hbm, wb_hbm, wu_hbm,
     out_ref, gb_ref, gc_ref,
     vol, cot, wc, wd, wb, wu, load_sem,
-    perm_xyz, perm_sub, perm_cot, perm_back, perm_out, perm_group, perm_rim, perm_brick, perm_part, lift_z,
+    perm_xyz, perm_sub, perm_cot, perm_back, perm_out, perm_group, perm_rim, perm_brick, lift_z,
     plane_z, face_main, take_main, face_y, take_y, face_x, take_x,
     padded, columns, turned, pre, cot_sub, slope_sub, hidden_sub,
     back_out, back_in, bricks, rims, shifted, rim_out, rim_in, corner_out, corner_in, pre_low,
@@ -214,8 +214,6 @@
     perm_sub[...] = selection(512, 512, sub_to_xyz)
     perm_back[...] = selection(512, 512, lambda r: sub_of_cell(r >> 6, (r >> 3) & 7, r & 7))
     perm_out[...] = selection(512, 512, lambda r: sub_of_cell((r >> 3) & 7, r & 7, r >> 6))
-
-    perm_part[...] = selection(128, 128, lambda r: ((r & 31) >> 2) * 16 + (r >> 5) * 4 + (r & 3))
 
     def shifted_z(r, shift, column_of):
         z = (r & 15) + shift
@@ -439,17 +437,6 @@
         weights = jnp.concatenate([wb[a * 9 + step] for a in range(3)], axis=1)
         part_acc[...] += matmul_nt(jnp.concatenate(windows, axis=1), weights)
 
-    part_copies = []
-
-    def send_parts(which, rows):
-        part_out[which] = matmul(perm_part[...], rows.astype(BF)).astype(BF).reshape(4, 32, 512)
-        for d in (1, 2, 3):
-            peer = around(gz, d, 4)
-            copy = remote(part_out.at[which, peer], part_in.at[which, d - 1], {"gz": peer})
-            copy.start()
-            part_copies.append(copy)
-
-    send_parts(0, part_acc[64:192])
     finish_gx(lambda: None, lambda: None)
     for a in range(3):
         for side, x in ((0, 0), (1, 5)):
@@ -463,7 +450,13 @@
             weights = jnp.concatenate([wb[a * 9 + 3 * b + c] for a in range(3)], axis=1)
             part_acc[rows : rows + 64] += matmul_nt(jnp.concatenate(windows, axis=1), weights)
 
-    send_parts(1, jnp.concatenate([part_acc[0:64], part_acc[192:256]], axis=0))
+    part_out[...] = matmul(perm_brick[...], part_acc[...].astype(BF)).astype(BF).reshape(4, 64, 512)
+    part_copies = []
+    for d in (1, 2, 3):
+        peer = around(gz, d, 4)
+        copy = remote(part_out.at[peer], part_in.at[d - 1], {"gz": peer})
+        copy.start()
+        part_copies.append(copy)
 
     bottle_taps(8, 13 + core, other)
     gb_first = remote(gb_all.at[pl.ds(other, 14)], gb_one, {"gy": gy ^ 1})
@@ -541,14 +534,10 @@
 
     for copy in part_copies:
         copy.wait()
-    sums = []
-    for which in range(2):
-        total = part_out[which, gz].astype(F32)
-        for d in range(3):
-            total = total + part_in[which, d].astype(F32)
-        sums.append(total)
-    inner, outer = sums
-    coarse_grad = jnp.concatenate([outer[0:16], inner, outer[16:32]], axis=0).astype(BF)
+    coarse_grad = part_out[gz].astype(F32)
+    for d in range(3):
+        coarse_grad = coarse_grad + part_in[d].astype(F32)
+    coarse_grad = coarse_grad.astype(BF)
     for s in range(8):
         rows = pl.ds(64 * s, 64)
         spread = matmul_nt(coarse_grad, wd[s]) + cot_sub[rows].astype(F32)
@@ -691,7 +680,7 @@
         kept(512, 128), kept(512, 128), kept(27, 128, 128), kept(8, 128, 512),
         kept(27, 512, 128), kept(8, 512, 128), pltpu.SemaphoreType.DMA((6,)),
         kept(512, 512), kept(512, 512), kept(512, 512), kept(512, 512), kept(512, 512),
-        kept(3, 256, 256), kept(3, 128, 128), kept(256, 256), kept(128, 128), kept(3, 128, 128),
+        kept(3, 256, 256), kept(3, 128, 128), kept(256, 256), kept(3, 128, 128),
         kept(2, 64, 128), kept(2, 64, 128), kept(2, 64, 128), kept(2, 80, 128), kept(2, 80, 128),
         kept(2, 48, 128), kept(2, 48, 128),
         vmem((10, 10, 24, 128), F32), kept(27, 512, 128), kept(32, 128, 512), vmem((512, 128), F32),
@@ -700,8 +689,8 @@
         kept(2, 64, 512), kept(2, 64, 512), kept(2, 32, 512), kept(4, 32, 512), vmem((256, 128), F32),
         kept(256, 128), kept(3, 6, 6, 16, 128), kept(2, 64, 128), kept(2, 64, 128),
         kept(2, 96, 128), kept(2, 128, 128),
-        kept(4, 64, 128), kept(4, 64, 128), vmem((256, 512), F32), kept(2, 4, 32, 512),
-        kept(2, 3, 32, 512), kept(512, 128),
+        kept(4, 64, 128), kept(4, 64, 128), vmem((256, 512), F32), kept(4, 64, 512),
+        kept(3, 64, 512), kept(512, 128),
         kept(28, 4, 2, 4, 16, 128), kept(14, 4, 2, 4, 16, 128),
         kept(3, 4, 2, 4, 16, 128), kept(3, 3, 2, 4, 16, 128), kept(3, 4, 4, 2, 16, 128), kept(3, 3, 4, 2, 16, 128),
         kept(7, 2, 4, 16, 128), kept(7, 4, 2, 16, 128),

time: 88.5 us -> 86.8 us (0.981)
  Pallas kernels: 86.8 us -> 85.9 us
where the time goes in v7:
time: 86.8 us; the launch traced here: 86.6 us
  Pallas kernels  85.9 us (99%)
    pallas_call x1, Pallas kernels, body(): pl.pallas_call(level_kernel, out_shape=(jax.ShapeDtypeStruct((512, 128),...  84.3 us

profile of v7, /device:TPU:1, one launch (start us, length us, event | category | flops | bytes accessed | tf_op | source)
XLA Modules:
  0.0 86.6 jit_solution(1167141450763956163)
XLA Ops:
  0.6 84.3 %level.1 = (bf16[512,128]{1,0:T(8,128)(2,1)}, f32[28,8,128]{2,1,0:T(8,128)}, f32[32,2,128]{2,1,0:T(2,128)}) custom-call(bf16[512,128]{1,0:T(8,128)(2,1)} %bitcast.9, bf16[512,128]{1,0:T(8,128)(2,1)} %bitcast.10, bf16[27,128,128]{2,1,0:T(8,128)(2,1)} %bitcast.8, bf16[8,128,512]{2,1,0:T(8,128)(2,1)} %wd_hbm.1, bf16[27,512,128]{2,1,0:T(8,128)(2,1)} %bitcast.7, ...), custom_call_target="tpu_custom_call" | custom-call | tf_op jit(solution)/shard_map/level/pallas_call | solution.py:704
  84.9 1.7 %deliver.1 = (bf16[512,128]{1,0:T(8,128)(2,1)}, f32[27,8,128]{2,1,0:T(8,128)}, f32[27,2,128]{2,1,0:T(2,128)}) custom-call(bf16[512,128]{1,0:T(8,128)(2,1)} %get-tuple-element.9.out_ref, f32[28,8,128]{2,1,0:T(8,128)} %get-tuple-element.10.gb_ref, f32[32,2,128]{2,1,0:T(2,128)} %get-tuple-element.11.gc_ref), custom_call_target="tpu_custom_call" | custom-call | tf_op jit(solution)/shard_map/deliver/pallas_call | solution.py:726
